TPU v7x, 32 devices: a whole 2x2x4 slice. The times are simulated.
32 devices in a mesh: grp: 2 (over x), row: 16 (over z, y, core).
Axes of the slice: x: 2, y: 2, z: 4, core: 2. Of those that a mesh axis runs over, the one named last changes fastest.
Arguments:
- positions: float32 [3, 12288], P(None, ('grp', 'row')), parts along dimension 1, may hold values from -6 to 6
- noise: float32 [3, 12288], P(None, ('grp', 'row')), parts along dimension 1, may hold values from -6 to 6
- atom_single: bfloat16 [12288, 128], P(('grp', 'row')), parts along dimension 0, may hold values from -6 to 6
- atom_token: int32 [12288], P(('grp', 'row')), parts along dimension 0, may hold values from 0 to 511, as said below
- atom_counts: int32 [32], P(('grp', 'row')), parts along dimension 0, may hold values from 192 to 384, as said below
- window_offsets: int32 [384], P(('grp', 'row')), parts along dimension 0, may hold values from -64 to -32
- atom_bias: float32 [4, 12288, 128], P(None, ('grp', 'row')), parts along dimension 1, may hold values from -4 to 302
- token_single: bfloat16 [1024, 768], P(('grp', 'row')), parts along dimension 0, may hold values from -6 to 6
- token_bias: float32 [16, 1024, 512], P(None, ('grp', 'row')), parts along dimension 1, may hold values from -9 to 302
- pair_mask: int32 [1024, 512], P(('grp', 'row')), parts along dimension 0, may hold values from 0 to 1, as said below
- w_coord: float32 [3, 128], replicated, may hold values from -3.5 to 3.5
- w_atom_qkv: bfloat16 [128, 384], replicated, may hold values from -0.5 to 0.5
- w_atom_out: bfloat16 [128, 128], replicated, may hold values from -0.5 to 0.5
- w_agg: bfloat16 [128, 768], replicated, may hold values from -0.5 to 0.5
- w_tok_qkv: bfloat16 [768, 2304], replicated, may hold values from -0.21875 to 0.21875
- w_tok_gate: bfloat16 [768, 768], replicated, may hold values from -0.21875 to 0.21875
- w_tok_out: bfloat16 [768, 768], replicated, may hold values from -0.21875 to 0.21875
- w_back: bfloat16 [768, 128], replicated, may hold values from -0.21875 to 0.21875
- w_pos: bfloat16 [3, 128], replicated, may hold values from -0.5 to 0.5
Outputs:
- denoised: float32 [3, 12288], P(None, ('grp', 'row')), parts along dimension 1
- token_out: bfloat16 [1024, 768], P(('grp', 'row')), parts along dimension 0
There are 2 independent parts, one for each index of `grp`. A program takes and returns all parts, laid end to end along the dimension named above; an argument that names none is the same for every part. Nothing has to cross between parts.
Inputs may be any that keep to these rules, and one draw needn't show every extreme that they name: `atom_token`: slots i * 384 to (i + 1) * 384 - 1 name tokens from i * 32 - 32 // 4 to (i + 1) * 32 + 32 // 4; ids never fall along the slots. `atom_counts`: entry i is the number of live slots at the front of slots i * 384 onward; some entry equals 384. `pair_mask`: each token's own column, and the column of its index xor 1, are 1.
All inputs are finite; a program needn't handle non-finite values.
Results may differ from a plain program's by a relative error of at most 0.0075.
Values may be sent and summed in bfloat16 or wider, within the bound.
A program may use at most 64 MiB of HBM per device.

v0:
```python
import jax
import jax.numpy as jnp
from jax import lax
from jax.experimental import pallas as pl
from jax.experimental.pallas import tpu as pltpu
from jax.sharding import PartitionSpec as P

AH = 4
TH = 16
QWIN = 32
KWIN = 128
BEHIND = KWIN // 2
AHEAD = KWIN - QWIN

noise_level = 2.0
input_scale = 1.0 / 5.0**0.5
skip_scale = 1.0 / 5.0
output_scale = 2.0 / 5.0**0.5
masked_score = -1e30

F32 = jnp.float32
BF16 = jnp.bfloat16
PIECES = 2


def normalize(values):
    center = values - jnp.mean(values, axis=-1, keepdims=True)
    spread = jnp.mean(center * center, axis=-1, keepdims=True)
    return center * lax.rsqrt(spread + 1e-05)


def mm(a, b):
    return jnp.dot(a, b, preferred_element_type=F32)


def mm_t(a, b):
    return lax.dot_general(a, b, (((1,), (1,)), ((), ())), preferred_element_type=F32)


def lanes_between(width, low, high):
    lane = lax.broadcasted_iota(jnp.int32, (1, width), 1)
    return ((lane >= low) & (lane < high)).astype(F32)


def kernel(
    n,
    counts_s, offsets_s,
    pos_h, noise_h, single_h, token_h, abias_h, tsingle_h, tbias_h, mask_h,
    wcoord_h, waqkv_h, waout_h, wagg_h, wtqkv_h, wgate_h, wtout_h, wback_h, wpos_h,
    den_ref, tout_ref,
    pos, noise, single, token, abias, tsingle, tbias, pmask,
    wcoord, waqkv, waout, wagg, wtqkv, wgate, wtout, wback, wpos,
    columns, hs, tail, head, lo, up, shifted, ext, keys_s, values_s, mid, att_s,
    part_down, part_up, from_low, from_high, u_all, near,
    local_sem, edge_send, edge_recv, line_send, ag_send, ag_recv,
):
    cap, ca = single.shape
    rows, ct = tsingle.shape
    me = lax.axis_index("row")
    last = n - 1
    has_low = me > 0
    has_high = me < last

    pairs = [
        (pos_h, pos), (noise_h, noise), (single_h, single), (wcoord_h, wcoord), (token_h, token),
        (waqkv_h, waqkv), (abias_h, abias), (waout_h, waout), (wagg_h, wagg), (tsingle_h, tsingle),
        (wtqkv_h, wtqkv), (wgate_h, wgate), (mask_h, pmask), (tbias_h, tbias), (wtout_h, wtout),
        (wback_h, wback), (wpos_h, wpos),
    ]
    copies = {}
    for k, (src, dst) in enumerate(pairs):
        copies[id(dst)] = pltpu.make_async_copy(src, dst, local_sem.at[k])
        copies[id(dst)].start()

    def need(*refs):
        for r in refs:
            copies[id(r)].wait()

    core = lax.rem(me, 2)
    y = lax.rem(me // 2, 2)
    z = me // 4
    depth = n // 4

    def index_of(zz, yy, cc):
        return zz * 4 + yy * 2 + cc

    partner = index_of(z, y, 1 - core)
    across = index_of(z, 1 - y, core)
    line = []
    for d in range(1, depth):
        line.append((z + d < depth, index_of(z + d, y, core), 2 * d))
        line.append((z >= d, index_of(z - d, y, core), 2 * d + 1))

    barrier = pltpu.get_barrier_semaphore()

    def greet(peer):
        pl.semaphore_signal(
            barrier, inc=1, device_id={"row": peer}, device_id_type=pl.DeviceIdType.MESH
        )

    greet(partner)
    greet(across)
    for there, peer, _ in line:
        pl.when(there)(lambda peer=peer: greet(peer))
    far = me - 1 + 2 * core
    has_far = (far >= 0) & (far < n)
    pl.when(has_far)(lambda: greet(far))

    live = jnp.clip(counts_s[0], cap // 2, cap)
    shifted[...] = jnp.zeros_like(shifted)
    columns[...] = jnp.zeros_like(columns)
    near[...] = jnp.zeros_like(near)

    @pl.when(me == 0)
    def _():
        lo[...] = jnp.zeros_like(lo)
        from_low[...] = jnp.zeros_like(from_low)

    @pl.when(me == last)
    def _():
        up[...] = jnp.zeros_like(up)
        from_high[...] = jnp.zeros_like(from_high)

    need(pos, noise, single, wcoord, token)
    noisy = pos[...] + noise_level * noise[...]
    columns[0:3, :] = input_scale * noisy
    relative = token[...].reshape(1, cap) - (me - 1) * rows
    columns[3:4, :] = relative.astype(F32)
    turned = columns[...].T
    wc = wcoord[...]
    atom_start = single[...].astype(F32) + (
        turned[:, 0:1] * wc[0:1, :] + turned[:, 1:2] * wc[1:2, :] + turned[:, 2:3] * wc[2:3, :]
    )
    near_rows = near.shape[0]
    lane_ids = lax.broadcasted_iota(jnp.int32, (cap, near_rows), 1).astype(F32)
    hot_t = (turned[:, 3:4] == lane_ids).astype(F32).astype(BF16)
    normed = normalize(atom_start)
    hs[...] = normed
    mid[...] = atom_start
    head[...] = normed[:AHEAD].astype(BF16)
    tail[...] = hs[pl.ds(live - BEHIND, BEHIND), :].astype(BF16)

    peers = 2 + (depth - 1) + jnp.where(has_far, 1, 0)
    pl.semaphore_wait(barrier, peers)

    def edge(k, src, dst, peer):
        return pltpu.make_async_remote_copy(
            src_ref=src,
            dst_ref=dst,
            send_sem=edge_send.at[k],
            recv_sem=edge_recv.at[k],
            device_id={"row": peer},
            device_id_type=pl.DeviceIdType.MESH,
        )

    def exchange(stage, src_up, dst_up, src_down, dst_down):
        going_up = edge(2 * stage, src_up, dst_up, me + 1)
        going_down = edge(2 * stage + 1, src_down, dst_down, me - 1)
        pl.when(has_high)(going_up.start)
        pl.when(has_low)(going_down.start)

        def receive():
            pl.when(has_low)(going_up.wait_recv)
            pl.when(has_high)(going_down.wait_recv)

        def finish():
            pl.when(has_high)(going_up.wait_send)
            pl.when(has_low)(going_down.wait_send)

        return receive, finish

    receive_rim, finish_rim = exchange(0, tail, lo, head, up)

    need(waqkv)
    queries = mm(normed.astype(BF16), waqkv[:, :ca]).astype(BF16)
    hw = ca // AH
    head_lanes = [lanes_between(ca, h * hw, (h + 1) * hw) for h in range(AH)]
    ext[BEHIND : BEHIND + cap, :] = normed
    need(abias)

    receive_rim()
    ext[:BEHIND, :] = lo[...].astype(F32)
    half = cap // 2
    shifted[half : half + AHEAD, :] = up[...].astype(F32)
    first = BEHIND + half
    count = half + AHEAD
    moved = shifted[pl.ds(cap - live, count), :]
    row_ids = lax.broadcasted_iota(jnp.int32, (count, ca), 0) + first
    ext[first : BEHIND + cap, :] = jnp.where(
        row_ids[:half] < BEHIND + live, ext[first : BEHIND + cap, :], moved[:half]
    )
    ext[BEHIND + cap :, :] = moved[half:]
    kv_rows = mm(ext[...].astype(BF16), waqkv[:, ca:]).astype(BF16).astype(F32)
    keys_s[...] = kv_rows[:, :ca]
    values_s[...] = kv_rows[:, ca:]

    top = jnp.where(has_high, BEHIND + live + AHEAD, BEHIND + live)
    bottom = jnp.where(has_low, 0, BEHIND)
    lane_key = lax.broadcasted_iota(jnp.int32, (1, KWIN), 1)
    for w in range(cap // QWIN):
        at = BEHIND + QWIN * w + offsets_s[w]
        key = keys_s[pl.ds(at, KWIN), :].astype(BF16)
        value = values_s[pl.ds(at, KWIN), :].astype(BF16)
        q = queries[w * QWIN : (w + 1) * QWIN, :]
        wide = jnp.concatenate([q * m.astype(BF16) for m in head_lanes], axis=0)
        score = mm_t(wide, key) * (1.0 / hw**0.5)
        score = score + abias[:, w * QWIN : (w + 1) * QWIN, :].reshape(AH * QWIN, KWIN)
        keys = lane_key + at
        score = jnp.where((keys >= bottom) & (keys < top), score, masked_score)
        e = jnp.exp(score - jnp.max(score, axis=-1, keepdims=True))
        weights = (e / jnp.sum(e, axis=-1, keepdims=True)).astype(BF16)
        out = mm(weights, value)
        total = out[:QWIN] * head_lanes[0]
        for h in range(1, AH):
            total = total + out[h * QWIN : (h + 1) * QWIN] * head_lanes[h]
        att_s[w * QWIN : (w + 1) * QWIN, :] = total.astype(BF16)

    need(waout, wagg)
    atom_mid = mid[...] + mm(att_s[...], waout[...])
    mid[...] = atom_mid
    spread = jnp.maximum(mm(atom_mid.astype(BF16), wagg[...]), 0.0).astype(BF16)
    slot_lane = lax.broadcasted_iota(jnp.int32, (1, cap), 1)
    living = slot_lane < live
    sub_ids = lax.broadcasted_iota(jnp.int32, (3 * rows, cap), 0)
    hot = ((sub_ids == relative) & living).astype(F32)
    counted = jnp.sum(hot, axis=-1, keepdims=True)
    partial = mm(hot.astype(BF16), spread)
    few = jnp.minimum(counted, 256.0)
    lane_c = lax.broadcasted_iota(jnp.int32, (3 * rows, 128), 1)
    count_wide = jnp.where(lane_c < 64, few, counted - few)
    part_down[:, :ct] = partial[:rows].astype(BF16)
    part_down[:, ct:] = count_wide[:rows].astype(BF16)
    part_up[:, :ct] = partial[2 * rows :].astype(BF16)
    part_up[:, ct:] = count_wide[2 * rows :].astype(BF16)
    receive_part, finish_part = exchange(1, part_up, from_low, part_down, from_high)

    need(tsingle, wtqkv, wgate)
    receive_part()
    low = from_low[...].astype(F32)
    high = from_high[...].astype(F32)
    token_sum = partial[rows : 2 * rows] + high[:, :ct] + low[:, :ct]
    token_count = (
        counted[rows : 2 * rows]
        + (high[:, ct : ct + 1] + high[:, ct + 64 : ct + 65])
        + (low[:, ct : ct + 1] + low[:, ct + 64 : ct + 65])
    )
    token_in = tsingle[...].astype(F32) + token_sum / jnp.maximum(token_count, 1.0)
    u = normalize(token_in).astype(BF16)
    u_all[pl.ds(pl.multiple_of(me * rows, rows), rows), :] = u

    part = rows // PIECES

    def block(src, piece, peer, sent):
        view = u_all.at[pl.ds(pl.multiple_of(src * rows + piece * part, part), part), :]
        return pltpu.make_async_remote_copy(
            src_ref=view,
            dst_ref=view,
            send_sem=sent,
            recv_sem=ag_recv.at[src, piece],
            device_id={"row": peer},
            device_id_type=pl.DeviceIdType.MESH,
        )

    def relay(src, piece, over, act):
        if over:
            act(block(src, piece, across, ag_send.at[0, src, piece]))
        act(block(src, piece, partner, ag_send.at[1, src, piece]))

    def own_sends(act):
        for piece in range(PIECES):
            relay(me, piece, True, act)
            for there, peer, way in line:
                pl.when(there)(lambda piece=piece, peer=peer, way=way: act(block(me, piece, peer, line_send.at[way, piece])))

    def start(c):
        c.start()

    def end(c):
        c.wait_send()

    steps = []
    for d in range(1, depth + 1):
        if d < depth:
            steps.append((z >= d, index_of(z - d, y, core), True))
            steps.append((z + d < depth, index_of(z + d, y, core), True))
        if d == 1:
            steps.append((None, across, False))
        else:
            steps.append((z >= d - 1, index_of(z - d + 1, 1 - y, core), False))
            steps.append((z + d - 1 < depth, index_of(z + d - 1, 1 - y, core), False))

    own_sends(start)

    tw = ct // TH
    group = TH // 2
    gw = group * tw
    tquery = mm(u, wtqkv[:, :ct]).astype(BF16)
    through = []
    group_lanes = [lanes_between(gw, h * tw, (h + 1) * tw) for h in range(group)]
    for g in range(2):
        q = tquery[:, g * gw : (g + 1) * gw]
        wide = jnp.concatenate([q * m.astype(BF16) for m in group_lanes], axis=0)
        through.append(mm_t(wide, wtqkv[:, ct + g * gw : ct + (g + 1) * gw]).astype(BF16))
    gate = jax.nn.sigmoid(mm(u, wgate[...]))

    def arrive(src, over):
        for piece in range(PIECES):
            block(src, piece, partner, ag_send.at[1, 0, piece]).wait_recv()
            relay(src, piece, over, start)

    def leave(src, over):
        for piece in range(PIECES):
            relay(src, piece, over, end)

    def each(visit):
        for there, src, over in steps:
            if there is None:
                visit(src, over)
            else:
                pl.when(there)(lambda src=src, over=over: visit(src, over))

    each(arrive)
    for zz in range(depth):
        for yy in range(2):
            for piece in range(PIECES):
                block(index_of(zz, yy, 1 - core), piece, partner, ag_send.at[1, 0, piece]).wait_recv()

    need(pmask, tbias, wtout, wback, wpos)
    features = u_all[...]
    allowed = (pmask[...] == 1)[None]
    pieces = []
    for g in range(2):
        score = mm_t(through[g], features) * (1.0 / tw**0.5)
        score = score.reshape(group, rows, score.shape[-1]) + tbias[g * group : (g + 1) * group]
        score = jnp.where(allowed, score, masked_score)
        e = jnp.exp(score - jnp.max(score, axis=-1, keepdims=True))
        weights = (e / jnp.sum(e, axis=-1, keepdims=True)).astype(BF16)
        mixed = mm(weights.reshape(group * rows, -1), features).astype(BF16)
        out = mm(mixed, wtqkv[:, 2 * ct + g * gw : 2 * ct + (g + 1) * gw])
        total = out[:rows] * group_lanes[0]
        for h in range(1, group):
            total = total + out[h * rows : (h + 1) * rows] * group_lanes[h]
        pieces.append(total)
    gated = (gate * jnp.concatenate(pieces, axis=1)).astype(BF16)
    token_out = (token_in + mm(gated, wtout[...])).astype(BF16)
    tout_ref[...] = token_out
    near[rows : 2 * rows, :] = mm(token_out, wback[...]).astype(BF16)
    own = near.at[rows : 2 * rows]
    receive_back, finish_back = exchange(
        2, own, near.at[0:rows], own, near.at[2 * rows : 3 * rows]
    )
    finish_rim()
    finish_part()
    own_sends(end)
    each(leave)
    receive_back()
    atom_last = mid[...] + mm(hot_t, near[...])
    final = normalize(atom_last).astype(BF16)
    update = mm_t(wpos[...], final)
    den_ref[...] = jnp.where(living, skip_scale * noisy + output_scale * update, 0.0)
    finish_back()


def on_device(
    positions, noise, atom_single, atom_token, atom_counts, window_offsets, atom_bias,
    token_single, token_bias, pair_mask, w_coord, w_atom_qkv, w_atom_out, w_agg,
    w_tok_qkv, w_tok_gate, w_tok_out, w_back, w_pos,
):
    n = lax.axis_size("row")
    cap, ca = atom_single.shape
    rows, ct = token_single.shape
    big = (
        positions, noise, atom_single, atom_token, atom_bias, token_single,
        token_bias, pair_mask, w_coord, w_atom_qkv, w_atom_out, w_agg, w_tok_qkv, w_tok_gate,
        w_tok_out, w_back, w_pos,
    )
    near_rows = -(-3 * rows // 128) * 128
    smem = pl.BlockSpec(memory_space=pltpu.SMEM)
    vmem = pl.BlockSpec(memory_space=pltpu.VMEM)
    return pl.pallas_call(
        lambda *refs: kernel(n, *refs),
        out_shape=(
            jax.ShapeDtypeStruct((positions.shape[0], cap), F32),
            jax.ShapeDtypeStruct((rows, ct), BF16),
        ),
        in_specs=[smem, smem] + [pl.BlockSpec(memory_space=pl.ANY)] * len(big),
        out_specs=(vmem, vmem),
        scratch_shapes=[pltpu.VMEM(a.shape, a.dtype) for a in big]
        + [
            pltpu.VMEM((128, cap), F32),
            pltpu.VMEM((cap, ca), F32),
            pltpu.VMEM((BEHIND, ca), BF16),
            pltpu.VMEM((AHEAD, ca), BF16),
            pltpu.VMEM((BEHIND, ca), BF16),
            pltpu.VMEM((AHEAD, ca), BF16),
            pltpu.VMEM((cap + AHEAD, ca), F32),
            pltpu.VMEM((BEHIND + cap + AHEAD, ca), F32),
            pltpu.VMEM((BEHIND + cap + AHEAD, ca), F32),
            pltpu.VMEM((BEHIND + cap + AHEAD, ca), F32),
            pltpu.VMEM((cap, ca), F32),
            pltpu.VMEM((cap, ca), BF16),
            pltpu.VMEM((rows, ct + 128), BF16),
            pltpu.VMEM((rows, ct + 128), BF16),
            pltpu.VMEM((rows, ct + 128), BF16),
            pltpu.VMEM((rows, ct + 128), BF16),
            pltpu.VMEM((n * rows, ct), BF16),
            pltpu.VMEM((near_rows, ca), BF16),
            pltpu.SemaphoreType.DMA((len(big),)),
            pltpu.SemaphoreType.DMA((6,)),
            pltpu.SemaphoreType.DMA((6,)),
            pltpu.SemaphoreType.DMA((n // 2, PIECES)),
            pltpu.SemaphoreType.DMA((2, n, PIECES)),
            pltpu.SemaphoreType.DMA((n, PIECES)),
        ],
        compiler_params=pltpu.CompilerParams(collective_id=0, has_side_effects=True),
    )(atom_counts, window_offsets, *big)


def solution(mesh):
    placed = (
        P(None, ("grp", "row")),
        P(None, ("grp", "row")),
        P(("grp", "row"), None),
        P(("grp", "row")),
        P(("grp", "row")),
        P(("grp", "row")),
        P(None, ("grp", "row"), None),
        P(("grp", "row"), None),
        P(None, ("grp", "row"), None),
        P(("grp", "row"), None),
    ) + (P(),) * 9
    return jax.shard_map(
        on_device,
        mesh=mesh,
        in_specs=placed,
        out_specs=(P(None, ("grp", "row")), P(("grp", "row"), None)),
        check_vma=False,
    )
```

profile of v0, /device:TPU:1, one launch (start us, length us, event | category | flops | bytes accessed | tf_op | source)
XLA Modules:
  0.0 36.6 jit_solution(18274818043533913317)
XLA Ops:
  1.3 32.6 %shard_map.194 = (f32[3,384]{1,0:T(4,128)}, bf16[32,768]{1,0:T(8,128)(2,1)}) custom-call(s32[1]{0:T(128)S(6)} %copy.23.refs_0_, s32[12]{0:T(128)} %refs_1_.1, f32[3,384]{1,0:T(4,128)} %refs_2_.1, f32[3,384]{1,0:T(4,128)} %refs_3_.1, bf16[384,128]{1,0:T(8,128)(2,1)} %refs_4_.1, s32[384]{0:T(512)} %refs_5_.1, f32[4,384,128]{2,1,0:T(8,128)} %refs_6_.1, ...), custom_call_target="tpu_custom_call" | custom-call | tf_op jit(solution)/shard_map/pallas_call | solution.py:380
  33.9 1.3 %copy.24 = f32[3,384]{1,0:T(4,128)} copy(f32[3,384]{1,0:T(4,128)} %get-tuple-element.4) | data formatting | bytes 9216
  35.2 1.4 %copy.25 = bf16[32,768]{1,0:T(8,128)(2,1)} copy(bf16[32,768]{1,0:T(8,128)(2,1)} %get-tuple-element.5) | data formatting | bytes 98304
where the time goes:
time: 36.8 us; the launch traced here: 36.6 us
  Pallas kernels  32.6 us (89%)
  local copies, waits for them, and re-layouts  2.71 us (7%)
  between operations  1.29 us (4%)
    pallas_call x1, Pallas kernels, on_device(): pl.pallas_call(lambda *refs: kernel(n, *refs), out_shape=(jax.ShapeDtypeS...  32.6 us
    unnamed x2, local copies, waits for them, and re-layouts  2.71 us

commit v1 on v0

--- a/solution.py
+++ b/solution.py
@@ -21,6 +21,7 @@
 F32 = jnp.float32
 BF16 = jnp.bfloat16
 PIECES = 2
+VMEM_LIMIT = 40 * 1024 * 1024
 
 
 def normalize(values):
@@ -44,10 +45,11 @@
 
 def kernel(
     n,
-    counts_s, offsets_s,
+    counts_s, offsets_h,
     pos_h, noise_h, single_h, token_h, abias_h, tsingle_h, tbias_h, mask_h,
     wcoord_h, waqkv_h, waout_h, wagg_h, wtqkv_h, wgate_h, wtout_h, wback_h, wpos_h,
     den_ref, tout_ref,
+    offsets_s,
     pos, noise, single, token, abias, tsingle, tbias, pmask,
     wcoord, waqkv, waout, wagg, wtqkv, wgate, wtout, wback, wpos,
     columns, hs, tail, head, lo, up, shifted, ext, keys_s, values_s, mid, att_s,
@@ -65,7 +67,7 @@
         (pos_h, pos), (noise_h, noise), (single_h, single), (wcoord_h, wcoord), (token_h, token),
         (waqkv_h, waqkv), (abias_h, abias), (waout_h, waout), (wagg_h, wagg), (tsingle_h, tsingle),
         (wtqkv_h, wtqkv), (wgate_h, wgate), (mask_h, pmask), (tbias_h, tbias), (wtout_h, wtout),
-        (wback_h, wback), (wpos_h, wpos),
+        (wback_h, wback), (wpos_h, wpos), (offsets_h, offsets_s),
     ]
     copies = {}
     for k, (src, dst) in enumerate(pairs):
@@ -106,7 +108,6 @@
     has_far = (far >= 0) & (far < n)
     pl.when(has_far)(lambda: greet(far))
 
-    live = jnp.clip(counts_s[0], cap // 2, cap)
     shifted[...] = jnp.zeros_like(shifted)
     columns[...] = jnp.zeros_like(columns)
     near[...] = jnp.zeros_like(near)
@@ -122,6 +123,7 @@
         from_high[...] = jnp.zeros_like(from_high)
 
     need(pos, noise, single, wcoord, token)
+    live = jnp.clip(counts_s[0], cap // 2, cap)
     noisy = pos[...] + noise_level * noise[...]
     columns[0:3, :] = input_scale * noisy
     relative = token[...].reshape(1, cap) - (me - 1) * rows
@@ -176,7 +178,7 @@
     hw = ca // AH
     head_lanes = [lanes_between(ca, h * hw, (h + 1) * hw) for h in range(AH)]
     ext[BEHIND : BEHIND + cap, :] = normed
-    need(abias)
+    need(abias, offsets_s)
 
     receive_rim()
     ext[:BEHIND, :] = lo[...].astype(F32)
@@ -361,6 +363,14 @@
     finish_back()
 
 
+def store(den, tout, den_h, tout_h, sem):
+    copies = [pltpu.make_async_copy(den, den_h, sem.at[0]), pltpu.make_async_copy(tout, tout_h, sem.at[1])]
+    for c in copies:
+        c.start()
+    for c in copies:
+        c.wait()
+
+
 def on_device(
     positions, noise, atom_single, atom_token, atom_counts, window_offsets, atom_bias,
     token_single, token_bias, pair_mask, w_coord, w_atom_qkv, w_atom_out, w_agg,
@@ -375,17 +385,16 @@
         w_tok_out, w_back, w_pos,
     )
     near_rows = -(-3 * rows // 128) * 128
-    smem = pl.BlockSpec(memory_space=pltpu.SMEM)
+    hbm = pl.BlockSpec(memory_space=pltpu.HBM)
     vmem = pl.BlockSpec(memory_space=pltpu.VMEM)
-    return pl.pallas_call(
+    out_shapes = (((positions.shape[0], cap), F32), ((rows, ct), BF16))
+    results = pl.pallas_call(
         lambda *refs: kernel(n, *refs),
-        out_shape=(
-            jax.ShapeDtypeStruct((positions.shape[0], cap), F32),
-            jax.ShapeDtypeStruct((rows, ct), BF16),
-        ),
-        in_specs=[smem, smem] + [pl.BlockSpec(memory_space=pl.ANY)] * len(big),
+        out_shape=tuple(pltpu.VMEM(shape, kind) for shape, kind in out_shapes),
+        in_specs=[pl.BlockSpec(memory_space=pltpu.SMEM)] + [hbm] * (1 + len(big)),
         out_specs=(vmem, vmem),
-        scratch_shapes=[pltpu.VMEM(a.shape, a.dtype) for a in big]
+        scratch_shapes=[pltpu.SMEM(window_offsets.shape, jnp.int32)]
+        + [pltpu.VMEM(a.shape, a.dtype) for a in big]
         + [
             pltpu.VMEM((128, cap), F32),
             pltpu.VMEM((cap, ca), F32),
@@ -405,15 +414,23 @@
             pltpu.VMEM((rows, ct + 128), BF16),
             pltpu.VMEM((n * rows, ct), BF16),
             pltpu.VMEM((near_rows, ca), BF16),
-            pltpu.SemaphoreType.DMA((len(big),)),
+            pltpu.SemaphoreType.DMA((1 + len(big),)),
             pltpu.SemaphoreType.DMA((6,)),
             pltpu.SemaphoreType.DMA((6,)),
             pltpu.SemaphoreType.DMA((n // 2, PIECES)),
             pltpu.SemaphoreType.DMA((2, n, PIECES)),
             pltpu.SemaphoreType.DMA((n, PIECES)),
         ],
-        compiler_params=pltpu.CompilerParams(collective_id=0, has_side_effects=True),
-    )(atom_counts, window_offsets, *big)
+        compiler_params=pltpu.CompilerParams(collective_id=0, has_side_effects=True, vmem_limit_bytes=VMEM_LIMIT),
+    )(atom_counts, *(pltpu.with_memory_space_constraint(a, pltpu.HBM) for a in (window_offsets,) + big))
+    results = tuple(pltpu.with_memory_space_constraint(a, pltpu.VMEM) for a in results)
+    return pl.pallas_call(
+        store,
+        out_shape=tuple(jax.ShapeDtypeStruct(shape, kind) for shape, kind in out_shapes),
+        in_specs=[vmem, vmem],
+        out_specs=(hbm, hbm),
+        scratch_shapes=[pltpu.SemaphoreType.DMA((2,))],
+    )(*results)
 
 
 def solution(mesh):

time: 36.8 us -> 33.5 us (0.910)
  local copies, waits for them, and re-layouts: 2.71 us -> 0 us
  Pallas kernels: 32.6 us -> 32 us
    unnamed x2 -> x0, local copies, waits for them, and re-layouts: 2.71 us -> none
    pallas_call x1 -> x2, Pallas kernels: 32.6 us -> 32 us  [the longest x1 31.3 us: on_device(): pl.pallas_call(lambda *refs: kernel(n, *refs), out_shape=tuple((pltpu.VME...]
where the time goes in v1:
time: 33.5 us; the launch traced here: 33.3 us
  Pallas kernels  32 us (96%)
  between operations  1.29 us (4%)
    pallas_call x1, Pallas kernels, on_device(): pl.pallas_call(lambda *refs: kernel(n, *refs), out_shape=tuple((pltpu.VME...  31.3 us

profile of v1, /device:TPU:1, one launch (start us, length us, event | category | flops | bytes accessed | tf_op | source)
XLA Modules:
  0.0 33.3 jit_solution(17321620305077147118)
XLA Ops:
  1.3 31.3 %shard_map.194 = (f32[3,384]{1,0:T(4,128)S(1)}, bf16[32,768]{1,0:T(8,128)(2,1)S(1)}) custom-call(s32[1]{0:T(128)S(6)} %copy.21.refs_0_, s32[12]{0:T(128)} %refs_1_.1, f32[3,384]{1,0:T(4,128)} %refs_2_.1, f32[3,384]{1,0:T(4,128)} %refs_3_.1, bf16[384,128]{1,0:T(8,128)(2,1)} %refs_4_.1, s32[384]{0:T(512)} %refs_5_.1, f32[4,384,128]{2,1,0:T(8,128)} %refs_6_.1, ...), custom_call_target="tpu_custom_call" | custom-call | tf_op jit(solution)/shard_map/pallas_call | solution.py:391
  32.6 0.6 %shard_map.195 = (f32[3,384]{1,0:T(4,128)}, bf16[32,768]{1,0:T(8,128)(2,1)}) custom-call(f32[3,384]{1,0:T(4,128)S(1)} %get-tuple-element.4.den, bf16[32,768]{1,0:T(8,128)(2,1)S(1)} %get-tuple-element.5.tout), custom_call_target="tpu_custom_call" | custom-call | tf_op jit(solution)/shard_map/pallas_call | solution.py:427

commit v2 on v1

--- a/solution.py
+++ b/solution.py
@@ -21,6 +21,7 @@
 F32 = jnp.float32
 BF16 = jnp.bfloat16
 PIECES = 2
+GROUP = 5
 VMEM_LIMIT = 40 * 1024 * 1024
 
 
@@ -174,48 +175,72 @@
     receive_rim, finish_rim = exchange(0, tail, lo, head, up)
 
     need(waqkv)
-    queries = mm(normed.astype(BF16), waqkv[:, :ca]).astype(BF16)
     hw = ca // AH
+    normed_b = normed.astype(BF16)
+    own = mm(normed_b, waqkv[...])
+    queries = (own[:, :ca] * (1.0 / hw**0.5)).astype(BF16)
     head_lanes = [lanes_between(ca, h * hw, (h + 1) * hw) for h in range(AH)]
+    keys_s[BEHIND : BEHIND + cap, :] = own[:, ca : 2 * ca]
+    values_s[BEHIND : BEHIND + cap, :] = own[:, 2 * ca :]
     ext[BEHIND : BEHIND + cap, :] = normed
     need(abias, offsets_s)
-
-    receive_rim()
-    ext[:BEHIND, :] = lo[...].astype(F32)
-    half = cap // 2
-    shifted[half : half + AHEAD, :] = up[...].astype(F32)
-    first = BEHIND + half
-    count = half + AHEAD
-    moved = shifted[pl.ds(cap - live, count), :]
-    row_ids = lax.broadcasted_iota(jnp.int32, (count, ca), 0) + first
-    ext[first : BEHIND + cap, :] = jnp.where(
-        row_ids[:half] < BEHIND + live, ext[first : BEHIND + cap, :], moved[:half]
-    )
-    ext[BEHIND + cap :, :] = moved[half:]
-    kv_rows = mm(ext[...].astype(BF16), waqkv[:, ca:]).astype(BF16).astype(F32)
-    keys_s[...] = kv_rows[:, :ca]
-    values_s[...] = kv_rows[:, ca:]
 
     top = jnp.where(has_high, BEHIND + live + AHEAD, BEHIND + live)
     bottom = jnp.where(has_low, 0, BEHIND)
     lane_key = lax.broadcasted_iota(jnp.int32, (1, KWIN), 1)
-    for w in range(cap // QWIN):
-        at = BEHIND + QWIN * w + offsets_s[w]
-        key = keys_s[pl.ds(at, KWIN), :].astype(BF16)
-        value = values_s[pl.ds(at, KWIN), :].astype(BF16)
-        q = queries[w * QWIN : (w + 1) * QWIN, :]
-        wide = jnp.concatenate([q * m.astype(BF16) for m in head_lanes], axis=0)
-        score = mm_t(wide, key) * (1.0 / hw**0.5)
-        score = score + abias[:, w * QWIN : (w + 1) * QWIN, :].reshape(AH * QWIN, KWIN)
-        keys = lane_key + at
-        score = jnp.where((keys >= bottom) & (keys < top), score, masked_score)
-        e = jnp.exp(score - jnp.max(score, axis=-1, keepdims=True))
-        weights = (e / jnp.sum(e, axis=-1, keepdims=True)).astype(BF16)
-        out = mm(weights, value)
-        total = out[:QWIN] * head_lanes[0]
-        for h in range(1, AH):
-            total = total + out[h * QWIN : (h + 1) * QWIN] * head_lanes[h]
-        att_s[w * QWIN : (w + 1) * QWIN, :] = total.astype(BF16)
+    ones = jnp.ones((KWIN, ca), BF16)
+
+    def attend(windows):
+        at = [BEHIND + QWIN * w + offsets_s[w] for w in windows]
+        scores = []
+        for w, start in zip(windows, at):
+            key = keys_s[pl.ds(start, KWIN), :].astype(BF16)
+            q = queries[w * QWIN : (w + 1) * QWIN, :]
+            wide = jnp.concatenate([q * m.astype(BF16) for m in head_lanes], axis=0)
+            scores.append(mm_t(wide, key))
+        exps = []
+        for w, start, score in zip(windows, at, scores):
+            score = score + abias[:, w * QWIN : (w + 1) * QWIN, :].reshape(AH * QWIN, KWIN)
+            keys = lane_key + start
+            score = jnp.where((keys >= bottom) & (keys < top), score, masked_score)
+            exps.append(jnp.exp(score - jnp.max(score, axis=-1, keepdims=True)).astype(BF16))
+        outs = []
+        for start, e in zip(at, exps):
+            value = values_s[pl.ds(start, KWIN), :].astype(BF16)
+            outs.append(mm(e, jnp.concatenate([value, ones], axis=1)))
+        for w, out in zip(windows, outs):
+            mixed = out[:QWIN] * wide_lanes[0]
+            for h in range(1, AH):
+                mixed = mixed + out[h * QWIN : (h + 1) * QWIN] * wide_lanes[h]
+            att_s[w * QWIN : (w + 1) * QWIN, :] = (mixed[:, :ca] / mixed[:, ca:]).astype(BF16)
+
+    wide_lanes = [jnp.concatenate([m, m], axis=1) for m in head_lanes]
+    half = cap // 2
+    count = cap // QWIN
+    behind_windows = BEHIND // QWIN
+    inner = [w for w in range(count) if w >= behind_windows and QWIN * w + AHEAD <= half]
+    outer = [w for w in range(count) if w not in inner]
+    attend(inner)
+
+    receive_rim()
+    ext[:BEHIND, :] = lo[...].astype(F32)
+    shifted[half : half + AHEAD, :] = up[...].astype(F32)
+    first = BEHIND + half
+    span = half + AHEAD
+    moved = shifted[pl.ds(cap - live, span), :]
+    row_ids = lax.broadcasted_iota(jnp.int32, (span, ca), 0) + first
+    ext[first : BEHIND + cap, :] = jnp.where(
+        row_ids[:half] < BEHIND + live, ext[first : BEHIND + cap, :], moved[:half]
+    )
+    ext[BEHIND + cap :, :] = moved[half:]
+    low_kv = mm(ext[:BEHIND, :].astype(BF16), waqkv[:, ca:])
+    keys_s[:BEHIND, :] = low_kv[:, :ca]
+    values_s[:BEHIND, :] = low_kv[:, ca:]
+    high_kv = mm(ext[first:, :].astype(BF16), waqkv[:, ca:])
+    keys_s[first:, :] = high_kv[:, :ca]
+    values_s[first:, :] = high_kv[:, ca:]
+    for k in range(0, len(outer), GROUP):
+        attend(outer[k : k + GROUP])
 
     need(waout, wagg)
     atom_mid = mid[...] + mm(att_s[...], waout[...])

time: 33.5 us -> 30.6 us (0.913)
  Pallas kernels: 32 us -> 29 us
    pallas_call x1, Pallas kernels: 31.3 us -> 28.4 us  [on_device(): pl.pallas_call(lambda *refs: kernel(n, *refs), out_shape=tuple((pltpu.VME...]
where the time goes in v2:
time: 30.6 us; the launch traced here: 30.3 us
  Pallas kernels  29 us (95%)
  between operations  1.29 us (4%)
    pallas_call x1, Pallas kernels, on_device(): pl.pallas_call(lambda *refs: kernel(n, *refs), out_shape=tuple((pltpu.VME...  28.4 us
    pallas_call x1, Pallas kernels, on_device(): pl.pallas_call(store, out_shape=tuple((jax.ShapeDtypeStruct(shape, kind)...  0.64 us

profile of v2, /device:TPU:1, one launch (start us, length us, event | category | flops | bytes accessed | tf_op | source)
XLA Modules:
  0.0 30.3 jit_solution(15885782958772110592)
XLA Ops:
  1.3 28.4 %shard_map.194 = (f32[3,384]{1,0:T(4,128)S(1)}, bf16[32,768]{1,0:T(8,128)(2,1)S(1)}) custom-call(s32[1]{0:T(128)S(6)} %copy.21.refs_0_, s32[12]{0:T(128)} %refs_1_.1, f32[3,384]{1,0:T(4,128)} %refs_2_.1, f32[3,384]{1,0:T(4,128)} %refs_3_.1, bf16[384,128]{1,0:T(8,128)(2,1)} %refs_4_.1, s32[384]{0:T(512)} %refs_5_.1, f32[4,384,128]{2,1,0:T(8,128)} %refs_6_.1, ...), custom_call_target="tpu_custom_call" | custom-call | tf_op jit(solution)/shard_map/pallas_call | solution.py:416
  29.7 0.6 %shard_map.195 = (f32[3,384]{1,0:T(4,128)}, bf16[32,768]{1,0:T(8,128)(2,1)}) custom-call(f32[3,384]{1,0:T(4,128)S(1)} %get-tuple-element.4.den, bf16[32,768]{1,0:T(8,128)(2,1)S(1)} %get-tuple-element.5.tout), custom_call_target="tpu_custom_call" | custom-call | tf_op jit(solution)/shard_map/pallas_call | solution.py:452

commit v3 on v2

--- a/solution.py
+++ b/solution.py
@@ -20,8 +20,8 @@
 
 F32 = jnp.float32
 BF16 = jnp.bfloat16
-PIECES = 2
 GROUP = 5
+BATCH = 4
 VMEM_LIMIT = 40 * 1024 * 1024
 
 
@@ -54,11 +54,13 @@
     pos, noise, single, token, abias, tsingle, tbias, pmask,
     wcoord, waqkv, waout, wagg, wtqkv, wgate, wtout, wback, wpos,
     columns, hs, tail, head, lo, up, shifted, ext, keys_s, values_s, mid, att_s,
-    part_down, part_up, from_low, from_high, u_all, near,
-    local_sem, edge_send, edge_recv, line_send, ag_send, ag_recv,
+    part_down, part_up, from_low, from_high, early_all, late_all, u_all, hot_s, near,
+    local_sem, edge_send, edge_recv, line_send, across_send, ag_send, ag_recv,
 ):
     cap, ca = single.shape
     rows, ct = tsingle.shape
+    margin = rows // 4
+    rim_rows = 2 * margin
     me = lax.axis_index("row")
     last = n - 1
     has_low = me > 0
@@ -91,8 +93,13 @@
     across = index_of(z, 1 - y, core)
     line = []
     for d in range(1, depth):
-        line.append((z + d < depth, index_of(z + d, y, core), 2 * d))
-        line.append((z >= d, index_of(z - d, y, core), 2 * d + 1))
+        line.append((z + d < depth, index_of(z + d, y, core), z + d))
+        line.append((z >= d, index_of(z - d, y, core), z - d))
+
+    ends = depth - 1
+    if ends:
+        line.append((z == 0, index_of(z + ends, 1 - y, core), z))
+        line.append((z == ends, index_of(z - ends, 1 - y, core), z))
 
     barrier = pltpu.get_barrier_semaphore()
 
@@ -128,22 +135,19 @@
     noisy = pos[...] + noise_level * noise[...]
     columns[0:3, :] = input_scale * noisy
     relative = token[...].reshape(1, cap) - (me - 1) * rows
-    columns[3:4, :] = relative.astype(F32)
     turned = columns[...].T
     wc = wcoord[...]
     atom_start = single[...].astype(F32) + (
         turned[:, 0:1] * wc[0:1, :] + turned[:, 1:2] * wc[1:2, :] + turned[:, 2:3] * wc[2:3, :]
     )
-    near_rows = near.shape[0]
-    lane_ids = lax.broadcasted_iota(jnp.int32, (cap, near_rows), 1).astype(F32)
-    hot_t = (turned[:, 3:4] == lane_ids).astype(F32).astype(BF16)
     normed = normalize(atom_start)
     hs[...] = normed
     mid[...] = atom_start
     head[...] = normed[:AHEAD].astype(BF16)
     tail[...] = hs[pl.ds(live - BEHIND, BEHIND), :].astype(BF16)
 
-    peers = 2 + (depth - 1) + jnp.where(has_far, 1, 0)
+    at_end = jnp.where((z == 0) | (z == ends), 1, 0) if ends else 0
+    peers = 2 + (depth - 1) + jnp.where(has_far, 1, 0) + at_end
     pl.semaphore_wait(barrier, peers)
 
     def edge(k, src, dst, peer):
@@ -251,53 +255,46 @@
     sub_ids = lax.broadcasted_iota(jnp.int32, (3 * rows, cap), 0)
     hot = ((sub_ids == relative) & living).astype(F32)
     counted = jnp.sum(hot, axis=-1, keepdims=True)
-    partial = mm(hot.astype(BF16), spread)
+    hot_s[...] = hot.astype(BF16)
+    partial = mm(hot_s[...], spread)
     few = jnp.minimum(counted, 256.0)
     lane_c = lax.broadcasted_iota(jnp.int32, (3 * rows, 128), 1)
     count_wide = jnp.where(lane_c < 64, few, counted - few)
-    part_down[:, :ct] = partial[:rows].astype(BF16)
-    part_down[:, ct:] = count_wide[:rows].astype(BF16)
-    part_up[:, :ct] = partial[2 * rows :].astype(BF16)
-    part_up[:, ct:] = count_wide[2 * rows :].astype(BF16)
+    down = slice(rows - margin, rows)
+    ahead = slice(2 * rows, 2 * rows + rim_rows)
+    part_down[:, :ct] = partial[down].astype(BF16)
+    part_down[:, ct:] = count_wide[down].astype(BF16)
+    part_up[:, :ct] = partial[ahead].astype(BF16)
+    part_up[:, ct:] = count_wide[ahead].astype(BF16)
     receive_part, finish_part = exchange(1, part_up, from_low, part_down, from_high)
 
-    need(tsingle, wtqkv, wgate)
-    receive_part()
-    low = from_low[...].astype(F32)
-    high = from_high[...].astype(F32)
-    token_sum = partial[rows : 2 * rows] + high[:, :ct] + low[:, :ct]
-    token_count = (
-        counted[rows : 2 * rows]
-        + (high[:, ct : ct + 1] + high[:, ct + 64 : ct + 65])
-        + (low[:, ct : ct + 1] + low[:, ct + 64 : ct + 65])
-    )
-    token_in = tsingle[...].astype(F32) + token_sum / jnp.maximum(token_count, 1.0)
-    u = normalize(token_in).astype(BF16)
-    u_all[pl.ds(pl.multiple_of(me * rows, rows), rows), :] = u
-
-    part = rows // PIECES
-
-    def block(src, piece, peer, sent):
-        view = u_all.at[pl.ds(pl.multiple_of(src * rows + piece * part, part), part), :]
+    need(tsingle)
+    own_sum = partial[rows : 2 * rows]
+    own_count = counted[rows : 2 * rows]
+    middle = slice(margin, rows - margin)
+    token_mid = tsingle[middle, :].astype(F32) + own_sum[middle] / jnp.maximum(own_count[middle], 1.0)
+    early_all[pl.ds(me, 1)] = normalize(token_mid).astype(BF16)[None]
+
+    def block(kind, src, peer, sent):
+        view = (early_all, late_all)[kind].at[src]
         return pltpu.make_async_remote_copy(
             src_ref=view,
             dst_ref=view,
             send_sem=sent,
-            recv_sem=ag_recv.at[src, piece],
+            recv_sem=ag_recv.at[src, kind],
             device_id={"row": peer},
             device_id_type=pl.DeviceIdType.MESH,
         )
 
-    def relay(src, piece, over, act):
+    def relay(kind, src, over, act):
         if over:
-            act(block(src, piece, across, ag_send.at[0, src, piece]))
-        act(block(src, piece, partner, ag_send.at[1, src, piece]))
-
-    def own_sends(act):
-        for piece in range(PIECES):
-            relay(me, piece, True, act)
-            for there, peer, way in line:
-                pl.when(there)(lambda piece=piece, peer=peer, way=way: act(block(me, piece, peer, line_send.at[way, piece])))
+            act(block(kind, src, across, across_send.at[src // 4, kind]))
+        act(block(kind, src, partner, ag_send.at[src // 2, kind]))
+
+    def own_sends(kind, act):
+        for there, peer, way in line:
+            pl.when(there)(lambda peer=peer, way=way: act(block(kind, me, peer, line_send.at[way, kind])))
+        relay(kind, me, True, act)
 
     def start(c):
         c.start()
@@ -305,85 +302,143 @@
     def end(c):
         c.wait_send()
 
-    steps = []
-    for d in range(1, depth + 1):
-        if d < depth:
-            steps.append((z >= d, index_of(z - d, y, core), True))
-            steps.append((z + d < depth, index_of(z + d, y, core), True))
-        if d == 1:
-            steps.append((None, across, False))
-        else:
-            steps.append((z >= d - 1, index_of(z - d + 1, 1 - y, core), False))
-            steps.append((z + d - 1 < depth, index_of(z + d - 1, 1 - y, core), False))
-
-    own_sends(start)
-
+    own_sends(0, start)
+
+    need(wtqkv, wgate)
+    receive_part()
+    low = from_low[...].astype(F32)
+    high = from_high[...].astype(F32)
+
+    def counts_in(sums):
+        return sums[:, ct : ct + 1] + sums[:, ct + 64 : ct + 65]
+
+    def edges(own, below, above):
+        return jnp.concatenate(
+            [own[:rim_rows] + below, own[rim_rows : rows - margin], own[rows - margin :] + above], axis=0
+        )
+
+    token_sum = edges(own_sum, low[:, :ct], high[:, :ct])
+    token_count = edges(own_count, counts_in(low), counts_in(high))
+    token_in = tsingle[...].astype(F32) + token_sum / jnp.maximum(token_count, 1.0)
+    u_wide = normalize(token_in)
+    u = u_wide.astype(BF16)
+    chunks = ct // 128
+    odd = [u_wide[margin : margin + 1, 128 * k : 128 * (k + 1)] for k in range(chunks)]
+    odd.append(jnp.zeros((rim_rows - chunks, 128), F32))
+    late = jnp.concatenate(
+        [
+            jnp.concatenate([u_wide[rows - margin :], u_wide[:margin]], axis=0),
+            jnp.concatenate(odd, axis=0),
+        ],
+        axis=1,
+    )
+    late_all[pl.ds(me, 1)] = late.astype(BF16)[None]
+    own_sends(1, start)
+
+    direct = []
+    crossed = []
+    for d in range(1, depth):
+        over = d < ends
+        direct.append((z >= d, index_of(z - d, y, core), over))
+        direct.append((z + d < depth, index_of(z + d, y, core), over))
+    crossed.append((None, across, False))
+    for d in range(1, depth):
+        crossed.append((z >= d, index_of(z - d, 1 - y, core), False))
+        crossed.append((z + d < depth, index_of(z + d, 1 - y, core), False))
+    steps = direct + crossed
+
+    def arrive(kind, src, over):
+        block(kind, src, partner, ag_send.at[0, kind]).wait_recv()
+        relay(kind, src, over, start)
+
+    def leave(kind, src, over):
+        relay(kind, src, over, end)
+
+    def each(kind, some, visit):
+        for there, src, over in some:
+            if there is None:
+                visit(kind, src, over)
+            else:
+                pl.when(there)(lambda src=src, over=over: visit(kind, src, over))
+
+    def last_hops(kind):
+        for zz in range(depth):
+            for yy in range(2):
+                block(kind, index_of(zz, yy, 1 - core), partner, ag_send.at[0, kind]).wait_recv()
+
+    each(0, direct[:2], arrive)
     tw = ct // TH
-    group = TH // 2
-    gw = group * tw
-    tquery = mm(u, wtqkv[:, :ct]).astype(BF16)
-    through = []
-    group_lanes = [lanes_between(gw, h * tw, (h + 1) * tw) for h in range(group)]
-    for g in range(2):
-        q = tquery[:, g * gw : (g + 1) * gw]
-        wide = jnp.concatenate([q * m.astype(BF16) for m in group_lanes], axis=0)
-        through.append(mm_t(wide, wtqkv[:, ct + g * gw : ct + (g + 1) * gw]).astype(BF16))
+    tquery = (mm(u, wtqkv[:, :ct]) * (1.0 / tw**0.5)).astype(BF16)
+    batches = []
+    for first_head in range(0, TH, BATCH):
+        heads = range(first_head, first_head + BATCH)
+        left = first_head * tw // 128 * 128
+        right = -(-(first_head + BATCH) * tw // 128) * 128
+        lanes = [lanes_between(right - left, h * tw - left, (h + 1) * tw - left) for h in heads]
+        q = tquery[:, left:right]
+        wide = jnp.concatenate([q * m.astype(BF16) for m in lanes], axis=0)
+        through = mm_t(wide, wtqkv[:, ct + left : ct + right]).astype(BF16)
+        batches.append((first_head, left, right, lanes, through))
     gate = jax.nn.sigmoid(mm(u, wgate[...]))
-
-    def arrive(src, over):
-        for piece in range(PIECES):
-            block(src, piece, partner, ag_send.at[1, 0, piece]).wait_recv()
-            relay(src, piece, over, start)
-
-    def leave(src, over):
-        for piece in range(PIECES):
-            relay(src, piece, over, end)
-
-    def each(visit):
-        for there, src, over in steps:
-            if there is None:
-                visit(src, over)
-            else:
-                pl.when(there)(lambda src=src, over=over: visit(src, over))
-
-    each(arrive)
-    for zz in range(depth):
-        for yy in range(2):
-            for piece in range(PIECES):
-                block(index_of(zz, yy, 1 - core), piece, partner, ag_send.at[1, 0, piece]).wait_recv()
-
+    mid_t = mid[...].T
+    each(0, direct[2:], arrive)
+    each(1, direct, arrive)
+    each(0, crossed, arrive)
+    each(1, crossed, arrive)
+    last_hops(0)
+    for src in range(n):
+        u_all[src * rows + margin : (src + 1) * rows - margin, :] = early_all[src]
+    last_hops(1)
+    first_row = lax.broadcasted_iota(jnp.int32, (margin, ct), 0) == 0
+    for src in range(n):
+        at = src * rows
+        u_all[at : at + margin, :] = late_all[src, margin:, :ct]
+        u_all[at + rows - margin : at + rows, :] = late_all[src, :margin, :ct]
+        extra = late_all[src, :, ct:].astype(F32)
+        row = jnp.concatenate([extra[k : k + 1] for k in range(chunks)], axis=1)
+        tile = early_all[src, :margin, :].astype(F32)
+        u_all[at + margin : at + 2 * margin, :] = jnp.where(first_row, row, tile).astype(BF16)
     need(pmask, tbias, wtout, wback, wpos)
     features = u_all[...]
     allowed = (pmask[...] == 1)[None]
-    pieces = []
-    for g in range(2):
-        score = mm_t(through[g], features) * (1.0 / tw**0.5)
-        score = score.reshape(group, rows, score.shape[-1]) + tbias[g * group : (g + 1) * group]
+    scores = [mm_t(through, features) for _, _, _, _, through in batches]
+    weighted = []
+    for (first_head, _, _, _, _), score in zip(batches, scores):
+        score = score.reshape(BATCH, rows, score.shape[-1]) + tbias[first_head : first_head + BATCH]
         score = jnp.where(allowed, score, masked_score)
         e = jnp.exp(score - jnp.max(score, axis=-1, keepdims=True))
         weights = (e / jnp.sum(e, axis=-1, keepdims=True)).astype(BF16)
-        mixed = mm(weights.reshape(group * rows, -1), features).astype(BF16)
-        out = mm(mixed, wtqkv[:, 2 * ct + g * gw : 2 * ct + (g + 1) * gw])
-        total = out[:rows] * group_lanes[0]
-        for h in range(1, group):
-            total = total + out[h * rows : (h + 1) * rows] * group_lanes[h]
-        pieces.append(total)
-    gated = (gate * jnp.concatenate(pieces, axis=1)).astype(BF16)
+        weighted.append(mm(weights.reshape(BATCH * rows, -1), features).astype(BF16))
+    blocks = [None] * chunks
+    for (_, left, right, lanes, _), mixed in zip(batches, weighted):
+        out = mm(mixed, wtqkv[:, 2 * ct + left : 2 * ct + right])
+        total = out[:rows] * lanes[0]
+        for h in range(1, BATCH):
+            total = total + out[h * rows : (h + 1) * rows] * lanes[h]
+        for k in range(left // 128, right // 128):
+            part = total[:, 128 * k - left : 128 * (k + 1) - left]
+            blocks[k] = part if blocks[k] is None else blocks[k] + part
+    gated = (gate * jnp.concatenate(blocks, axis=1)).astype(BF16)
     token_out = (token_in + mm(gated, wtout[...])).astype(BF16)
     tout_ref[...] = token_out
     near[rows : 2 * rows, :] = mm(token_out, wback[...]).astype(BF16)
-    own = near.at[rows : 2 * rows]
+    upper = near.at[2 * rows - margin : 2 * rows]
+    lower = near.at[rows : rows + rim_rows]
     receive_back, finish_back = exchange(
-        2, own, near.at[0:rows], own, near.at[2 * rows : 3 * rows]
+        2, upper, near.at[rows - margin : rows], lower, near.at[2 * rows : 2 * rows + rim_rows]
     )
     finish_rim()
     finish_part()
-    own_sends(end)
-    each(leave)
+    for kind in range(2):
+        own_sends(kind, end)
+        each(kind, steps, leave)
     receive_back()
-    atom_last = mid[...] + mm(hot_t, near[...])
-    final = normalize(atom_last).astype(BF16)
-    update = mm_t(wpos[...], final)
+    back_t = lax.dot_general(near[...], hot_s[...], (((0,), (0,)), ((), ())), preferred_element_type=F32)
+    atom_last = mid_t + back_t
+    center = atom_last - jnp.mean(atom_last, axis=0, keepdims=True)
+    width = jnp.mean(center * center, axis=0, keepdims=True)
+    final = (center * lax.rsqrt(width + 1e-05)).astype(BF16)
+    update = mm(wpos[...], final)
     den_ref[...] = jnp.where(living, skip_scale * noisy + output_scale * update, 0.0)
     finish_back()
 
@@ -409,7 +464,8 @@
         token_bias, pair_mask, w_coord, w_atom_qkv, w_atom_out, w_agg, w_tok_qkv, w_tok_gate,
         w_tok_out, w_back, w_pos,
     )
-    near_rows = -(-3 * rows // 128) * 128
+    margin = rows // 4
+    send_up, send_down = (2 * margin, ct + 128), (margin, ct + 128)
     hbm = pl.BlockSpec(memory_space=pltpu.HBM)
     vmem = pl.BlockSpec(memory_space=pltpu.VMEM)
     out_shapes = (((positions.shape[0], cap), F32), ((rows, ct), BF16))
@@ -433,18 +489,22 @@
             pltpu.VMEM((BEHIND + cap + AHEAD, ca), F32),
             pltpu.VMEM((cap, ca), F32),
             pltpu.VMEM((cap, ca), BF16),
-            pltpu.VMEM((rows, ct + 128), BF16),
-            pltpu.VMEM((rows, ct + 128), BF16),
-            pltpu.VMEM((rows, ct + 128), BF16),
-            pltpu.VMEM((rows, ct + 128), BF16),
+            pltpu.VMEM(send_down, BF16),
+            pltpu.VMEM(send_up, BF16),
+            pltpu.VMEM(send_up, BF16),
+            pltpu.VMEM(send_down, BF16),
+            pltpu.VMEM((n, rows - 2 * margin, ct), BF16),
+            pltpu.VMEM((n, 2 * margin, ct + 128), BF16),
             pltpu.VMEM((n * rows, ct), BF16),
-            pltpu.VMEM((near_rows, ca), BF16),
+            pltpu.VMEM((3 * rows, cap), BF16),
+            pltpu.VMEM((3 * rows, ca), BF16),
             pltpu.SemaphoreType.DMA((1 + len(big),)),
             pltpu.SemaphoreType.DMA((6,)),
             pltpu.SemaphoreType.DMA((6,)),
-            pltpu.SemaphoreType.DMA((n // 2, PIECES)),
-            pltpu.SemaphoreType.DMA((2, n, PIECES)),
-            pltpu.SemaphoreType.DMA((n, PIECES)),
+            pltpu.SemaphoreType.DMA((n // 4, 2)),
+            pltpu.SemaphoreType.DMA((n // 4, 2)),
+            pltpu.SemaphoreType.DMA((n // 2, 2)),
+            pltpu.SemaphoreType.DMA((n, 2)),
         ],
         compiler_params=pltpu.CompilerParams(collective_id=0, has_side_effects=True, vmem_limit_bytes=VMEM_LIMIT),
     )(atom_counts, *(pltpu.with_memory_space_constraint(a, pltpu.HBM) for a in (window_offsets,) + big))

time: 30.6 us -> 28.2 us (0.922)
  Pallas kernels: 29 us -> 26.7 us
    pallas_call x1, Pallas kernels: 28.4 us -> 26 us  [on_device(): pl.pallas_call(lambda *refs: kernel(n, *refs), out_shape=tuple((pltpu.VME...]
where the time goes in v3:
time: 28.2 us; the launch traced here: 28 us
  Pallas kernels  26.7 us (95%)
  between operations  1.29 us (5%)
    pallas_call x1, Pallas kernels, on_device(): pl.pallas_call(lambda *refs: kernel(n, *refs), out_shape=tuple((pltpu.VME...  26 us
    pallas_call x1, Pallas kernels, on_device(): pl.pallas_call(store, out_shape=tuple((jax.ShapeDtypeStruct(shape, kind)...  0.64 us

profile of v3, /device:TPU:1, one launch (start us, length us, event | category | flops | bytes accessed | tf_op | source)
XLA Modules:
  0.0 28.0 jit_solution(7183142544642128759)
XLA Ops:
  1.3 26.0 %shard_map.194 = (f32[3,384]{1,0:T(4,128)S(1)}, bf16[32,768]{1,0:T(8,128)(2,1)S(1)}) custom-call(s32[1]{0:T(128)S(6)} %copy.21.refs_0_, s32[12]{0:T(128)} %refs_1_.1, f32[3,384]{1,0:T(4,128)} %refs_2_.1, f32[3,384]{1,0:T(4,128)} %refs_3_.1, bf16[384,128]{1,0:T(8,128)(2,1)} %refs_4_.1, s32[384]{0:T(512)} %refs_5_.1, f32[4,384,128]{2,1,0:T(8,128)} %refs_6_.1, ...), custom_call_target="tpu_custom_call" | custom-call | tf_op jit(solution)/shard_map/pallas_call | solution.py:472
  27.3 0.6 %shard_map.195 = (f32[3,384]{1,0:T(4,128)}, bf16[32,768]{1,0:T(8,128)(2,1)}) custom-call(f32[3,384]{1,0:T(4,128)S(1)} %get-tuple-element.4.den, bf16[32,768]{1,0:T(8,128)(2,1)S(1)} %get-tuple-element.5.tout), custom_call_target="tpu_custom_call" | custom-call | tf_op jit(solution)/shard_map/pallas_call | solution.py:512

commit v4 on v3

--- a/solution.py
+++ b/solution.py
@@ -54,7 +54,7 @@
     pos, noise, single, token, abias, tsingle, tbias, pmask,
     wcoord, waqkv, waout, wagg, wtqkv, wgate, wtout, wback, wpos,
     columns, hs, tail, head, lo, up, shifted, ext, keys_s, values_s, mid, att_s,
-    part_down, part_up, from_low, from_high, early_all, late_all, u_all, hot_s, near,
+    part_down, part_up, from_low, from_high, early_all, late_all, u_half, bias_half, own_out, hot_s, near,
     local_sem, edge_send, edge_recv, line_send, across_send, ag_send, ag_recv,
 ):
     cap, ca = single.shape
@@ -304,6 +304,19 @@
 
     own_sends(0, start)
 
+    need(pmask, tbias)
+    pair = 2 * rows
+    allowed = pmask[...] == 1
+    front = lax.broadcasted_iota(jnp.int32, (1, 2 * pair), 1) < pair
+    for h in range(TH):
+        masked = jnp.where(allowed, tbias[h], masked_score)
+        for k in range(depth // 2):
+            one = masked[:, 4 * k * pair : (4 * k + 2) * pair]
+            two = masked[:, (4 * k + 2) * pair : (4 * k + 4) * pair]
+            here = slice(2 * k * pair, (2 * k + 2) * pair)
+            bias_half[0, h, :, here] = jnp.where(front, one, pltpu.roll(two, pair, 1))
+            bias_half[1, h, :, here] = jnp.where(front, pltpu.roll(one, pair, 1), two)
+    mid_t = mid[...].T
     need(wtqkv, wgate)
     receive_part()
     low = from_low[...].astype(F32)
@@ -361,10 +374,27 @@
             else:
                 pl.when(there)(lambda src=src, over=over: visit(kind, src, over))
 
-    def last_hops(kind):
+    def last_hops(column):
         for zz in range(depth):
-            for yy in range(2):
-                block(kind, index_of(zz, yy, 1 - core), partner, ag_send.at[0, kind]).wait_recv()
+            for kind in range(2):
+                block(kind, index_of(zz, column, 1 - core), partner, ag_send.at[0, kind]).wait_recv()
+
+    first_row = lax.broadcasted_iota(jnp.int32, (margin, ct), 0) == 0
+
+    def assemble(side, column):
+        for zz in range(depth):
+            for cc in range(2):
+                src = index_of(zz, column, cc)
+                at = (2 * zz + cc) * rows
+                early_rows = early_all[src]
+                late_rows = late_all[src]
+                u_half[side, at : at + margin, :] = late_rows[margin:, :ct]
+                u_half[side, at + rows - margin : at + rows, :] = late_rows[:margin, :ct]
+                extra = late_rows[:, ct:].astype(F32)
+                row = jnp.concatenate([extra[k : k + 1] for k in range(chunks)], axis=1)
+                tile = early_rows[:margin].astype(F32)
+                u_half[side, at + margin : at + 2 * margin, :] = jnp.where(first_row, row, tile).astype(BF16)
+                u_half[side, at + 2 * margin : at + rows - margin, :] = early_rows[margin:]
 
     each(0, direct[:2], arrive)
     tw = ct // TH
@@ -380,44 +410,52 @@
         through = mm_t(wide, wtqkv[:, ct + left : ct + right]).astype(BF16)
         batches.append((first_head, left, right, lanes, through))
     gate = jax.nn.sigmoid(mm(u, wgate[...]))
-    mid_t = mid[...].T
     each(0, direct[2:], arrive)
     each(1, direct, arrive)
+    last_hops(y)
+    assemble(0, y)
+
+    def scored(side, column):
+        features = u_half[side]
+        bias = bias_half[column]
+        scores = []
+        for first_head, _, _, _, through in batches:
+            score = mm_t(through, features)
+            scores.append(score + bias[first_head : first_head + BATCH].reshape(score.shape))
+        return features, scores
+
+    def valued(features, exps):
+        mixed = [mm(e.astype(BF16), features).astype(BF16) for e in exps]
+        return [
+            mm(m, wtqkv[:, 2 * ct + left : 2 * ct + right]) for m, (_, left, right, _, _) in zip(mixed, batches)
+        ]
+
+    features, scores = scored(0, y)
+    own_max = [jnp.max(score, axis=-1, keepdims=True) for score in scores]
+    exps = [jnp.exp(score - m) for score, m in zip(scores, own_max)]
+    own_total = [jnp.sum(e, axis=-1, keepdims=True) for e in exps]
+    for k, out in enumerate(valued(features, exps)):
+        own_out[k] = out
     each(0, crossed, arrive)
     each(1, crossed, arrive)
-    last_hops(0)
-    for src in range(n):
-        u_all[src * rows + margin : (src + 1) * rows - margin, :] = early_all[src]
-    last_hops(1)
-    first_row = lax.broadcasted_iota(jnp.int32, (margin, ct), 0) == 0
-    for src in range(n):
-        at = src * rows
-        u_all[at : at + margin, :] = late_all[src, margin:, :ct]
-        u_all[at + rows - margin : at + rows, :] = late_all[src, :margin, :ct]
-        extra = late_all[src, :, ct:].astype(F32)
-        row = jnp.concatenate([extra[k : k + 1] for k in range(chunks)], axis=1)
-        tile = early_all[src, :margin, :].astype(F32)
-        u_all[at + margin : at + 2 * margin, :] = jnp.where(first_row, row, tile).astype(BF16)
-    need(pmask, tbias, wtout, wback, wpos)
-    features = u_all[...]
-    allowed = (pmask[...] == 1)[None]
-    scores = [mm_t(through, features) for _, _, _, _, through in batches]
-    weighted = []
-    for (first_head, _, _, _, _), score in zip(batches, scores):
-        score = score.reshape(BATCH, rows, score.shape[-1]) + tbias[first_head : first_head + BATCH]
-        score = jnp.where(allowed, score, masked_score)
-        e = jnp.exp(score - jnp.max(score, axis=-1, keepdims=True))
-        weights = (e / jnp.sum(e, axis=-1, keepdims=True)).astype(BF16)
-        weighted.append(mm(weights.reshape(BATCH * rows, -1), features).astype(BF16))
+    last_hops(1 - y)
+    assemble(1, 1 - y)
+    need(wtout, wback, wpos)
+    features, scores = scored(1, 1 - y)
+    all_max = [jnp.maximum(m, jnp.max(score, axis=-1, keepdims=True)) for score, m in zip(scores, own_max)]
+    exps = [jnp.exp(score - m) for score, m in zip(scores, all_max)]
+    outs = valued(features, exps)
     blocks = [None] * chunks
-    for (_, left, right, lanes, _), mixed in zip(batches, weighted):
-        out = mm(mixed, wtqkv[:, 2 * ct + left : 2 * ct + right])
+    for k, (_, left, right, lanes, _) in enumerate(batches):
+        scale = jnp.exp(own_max[k] - all_max[k])
+        share = 1.0 / (own_total[k] * scale + jnp.sum(exps[k], axis=-1, keepdims=True))
+        out = own_out[k] * (scale * share) + outs[k] * share
         total = out[:rows] * lanes[0]
         for h in range(1, BATCH):
             total = total + out[h * rows : (h + 1) * rows] * lanes[h]
-        for k in range(left // 128, right // 128):
-            part = total[:, 128 * k - left : 128 * (k + 1) - left]
-            blocks[k] = part if blocks[k] is None else blocks[k] + part
+        for c in range(left // 128, right // 128):
+            part = total[:, 128 * c - left : 128 * (c + 1) - left]
+            blocks[c] = part if blocks[c] is None else blocks[c] + part
     gated = (gate * jnp.concatenate(blocks, axis=1)).astype(BF16)
     token_out = (token_in + mm(gated, wtout[...])).astype(BF16)
     tout_ref[...] = token_out
@@ -495,7 +533,9 @@
             pltpu.VMEM(send_down, BF16),
             pltpu.VMEM((n, rows - 2 * margin, ct), BF16),
             pltpu.VMEM((n, 2 * margin, ct + 128), BF16),
-            pltpu.VMEM((n * rows, ct), BF16),
+            pltpu.VMEM((2, n * rows // 2, ct), BF16),
+            pltpu.VMEM((2, TH, rows, n * rows // 2), F32),
+            pltpu.VMEM((TH // BATCH, BATCH * rows, 256), F32),
             pltpu.VMEM((3 * rows, cap), BF16),
             pltpu.VMEM((3 * rows, ca), BF16),
             pltpu.SemaphoreType.DMA((1 + len(big),)),

time: 28.2 us -> 27.5 us (0.975)
  Pallas kernels: 26.7 us -> 26 us
    pallas_call x1, Pallas kernels: 26 us -> 25.4 us  [on_device(): pl.pallas_call(lambda *refs: kernel(n, *refs), out_shape=tuple((pltpu.VME...]
where the time goes in v4:
time: 27.5 us; the launch traced here: 27.3 us
  Pallas kernels  26 us (95%)
  between operations  1.29 us (5%)
    pallas_call x1, Pallas kernels, on_device(): pl.pallas_call(lambda *refs: kernel(n, *refs), out_shape=tuple((pltpu.VME...  25.4 us
    pallas_call x1, Pallas kernels, on_device(): pl.pallas_call(store, out_shape=tuple((jax.ShapeDtypeStruct(shape, kind)...  0.64 us

profile of v4, /device:TPU:1, one launch (start us, length us, event | category | flops | bytes accessed | tf_op | source)
XLA Modules:
  0.0 27.3 jit_solution(14286191995116822)
XLA Ops:
  1.3 25.4 %shard_map.194 = (f32[3,384]{1,0:T(4,128)S(1)}, bf16[32,768]{1,0:T(8,128)(2,1)S(1)}) custom-call(s32[1]{0:T(128)S(6)} %copy.21.refs_0_, s32[12]{0:T(128)} %refs_1_.1, f32[3,384]{1,0:T(4,128)} %refs_2_.1, f32[3,384]{1,0:T(4,128)} %refs_3_.1, bf16[384,128]{1,0:T(8,128)(2,1)} %refs_4_.1, s32[384]{0:T(512)} %refs_5_.1, f32[4,384,128]{2,1,0:T(8,128)} %refs_6_.1, ...), custom_call_target="tpu_custom_call" | custom-call | tf_op jit(solution)/shard_map/pallas_call | solution.py:510
  26.7 0.6 %shard_map.195 = (f32[3,384]{1,0:T(4,128)}, bf16[32,768]{1,0:T(8,128)(2,1)}) custom-call(f32[3,384]{1,0:T(4,128)S(1)} %get-tuple-element.4.den, bf16[32,768]{1,0:T(8,128)(2,1)S(1)} %get-tuple-element.5.tout), custom_call_target="tpu_custom_call" | custom-call | tf_op jit(solution)/shard_map/pallas_call | solution.py:552

commit v5 on v4

--- a/solution.py
+++ b/solution.py
@@ -20,7 +20,7 @@
 
 F32 = jnp.float32
 BF16 = jnp.bfloat16
-GROUP = 5
+GROUP = 4
 BATCH = 4
 VMEM_LIMIT = 40 * 1024 * 1024
 
@@ -53,9 +53,9 @@
     offsets_s,
     pos, noise, single, token, abias, tsingle, tbias, pmask,
     wcoord, waqkv, waout, wagg, wtqkv, wgate, wtout, wback, wpos,
-    columns, hs, tail, head, lo, up, shifted, ext, keys_s, values_s, mid, att_s,
-    part_down, part_up, from_low, from_high, early_all, late_all, u_half, bias_half, own_out, hot_s, near,
-    local_sem, edge_send, edge_recv, line_send, across_send, ag_send, ag_recv,
+    columns, hs, tail, head, lo, up, shifted, queries, keys_s, values_s, mid, att_s,
+    part_down, part_up, from_low, from_high, early_all, late_all, u_half, bias_half, hot_s, near,
+    local_sem, edge_recv, line_recv, cross_early, cross_late, pair_recv, ready,
 ):
     cap, ca = single.shape
     rows, ct = tsingle.shape
@@ -93,13 +93,13 @@
     across = index_of(z, 1 - y, core)
     line = []
     for d in range(1, depth):
-        line.append((z + d < depth, index_of(z + d, y, core), z + d))
-        line.append((z >= d, index_of(z - d, y, core), z - d))
+        line.append((z + d < depth, index_of(z + d, y, core), False))
+        line.append((z >= d, index_of(z - d, y, core), False))
 
     ends = depth - 1
     if ends:
-        line.append((z == 0, index_of(z + ends, 1 - y, core), z))
-        line.append((z == ends, index_of(z - ends, 1 - y, core), z))
+        line.append((z == 0, index_of(z + ends, 1 - y, core), True))
+        line.append((z == ends, index_of(z - ends, 1 - y, core), True))
 
     barrier = pltpu.get_barrier_semaphore()
 
@@ -110,7 +110,8 @@
 
     greet(partner)
     greet(across)
-    for there, peer, _ in line:
+    beside = [(z >= 1, index_of(z - 1, y, core)), (z + 1 < depth, index_of(z + 1, y, core))]
+    for there, peer in beside:
         pl.when(there)(lambda peer=peer: greet(peer))
     far = me - 1 + 2 * core
     has_far = (far >= 0) & (far < n)
@@ -146,48 +147,65 @@
     head[...] = normed[:AHEAD].astype(BF16)
     tail[...] = hs[pl.ds(live - BEHIND, BEHIND), :].astype(BF16)
 
-    at_end = jnp.where((z == 0) | (z == ends), 1, 0) if ends else 0
-    peers = 2 + (depth - 1) + jnp.where(has_far, 1, 0) + at_end
+    links = jnp.where(z >= 1, 1, 0) + jnp.where(z + 1 < depth, 1, 0) + 1
+    peers = 1 + links + jnp.where(has_far, 1, 0)
     pl.semaphore_wait(barrier, peers)
 
-    def edge(k, src, dst, peer):
+    def edge(stage, way, src, dst, peer):
         return pltpu.make_async_remote_copy(
             src_ref=src,
             dst_ref=dst,
-            send_sem=edge_send.at[k],
-            recv_sem=edge_recv.at[k],
+            send_sem=local_sem.at[2 + way],
+            recv_sem=edge_recv.at[2 * (stage % 2) + way],
             device_id={"row": peer},
             device_id_type=pl.DeviceIdType.MESH,
         )
 
     def exchange(stage, src_up, dst_up, src_down, dst_down):
-        going_up = edge(2 * stage, src_up, dst_up, me + 1)
-        going_down = edge(2 * stage + 1, src_down, dst_down, me - 1)
+        going_up = edge(stage, 0, src_up, dst_up, me + 1)
+        going_down = edge(stage, 1, src_down, dst_down, me - 1)
         pl.when(has_high)(going_up.start)
         pl.when(has_low)(going_down.start)
 
-        def receive():
+        def receive_low():
             pl.when(has_low)(going_up.wait_recv)
+
+        def receive_high():
             pl.when(has_high)(going_down.wait_recv)
 
         def finish():
             pl.when(has_high)(going_up.wait_send)
             pl.when(has_low)(going_down.wait_send)
 
-        return receive, finish
-
-    receive_rim, finish_rim = exchange(0, tail, lo, head, up)
-
+        return receive_low, receive_high, finish
+
+    rim_low, rim_high, finish_rim = exchange(0, tail, lo, head, up)
+
+    def tell(step):
+        def one(peer):
+            pl.semaphore_signal(
+                ready.at[step], inc=1, device_id={"row": peer}, device_id_type=pl.DeviceIdType.MESH
+            )
+
+        one(across)
+        for there, peer in beside:
+            pl.when(there)(lambda peer=peer: one(peer))
+
+    def hear(step):
+        pl.semaphore_wait(ready.at[step], links)
+
+    rounds = depth - 1
+    if rounds:
+        tell(0)
     need(waqkv)
     hw = ca // AH
     normed_b = normed.astype(BF16)
     own = mm(normed_b, waqkv[...])
-    queries = (own[:, :ca] * (1.0 / hw**0.5)).astype(BF16)
+    queries[...] = (own[:, :ca] * (1.0 / hw**0.5)).astype(BF16)
     head_lanes = [lanes_between(ca, h * hw, (h + 1) * hw) for h in range(AH)]
     keys_s[BEHIND : BEHIND + cap, :] = own[:, ca : 2 * ca]
     values_s[BEHIND : BEHIND + cap, :] = own[:, 2 * ca :]
-    ext[BEHIND : BEHIND + cap, :] = normed
-    need(abias, offsets_s)
+    need(abias, offsets_s, waout, wagg)
 
     top = jnp.where(has_high, BEHIND + live + AHEAD, BEHIND + live)
     bottom = jnp.where(has_low, 0, BEHIND)
@@ -223,30 +241,42 @@
     count = cap // QWIN
     behind_windows = BEHIND // QWIN
     inner = [w for w in range(count) if w >= behind_windows and QWIN * w + AHEAD <= half]
-    outer = [w for w in range(count) if w not in inner]
-    attend(inner)
-
-    receive_rim()
-    ext[:BEHIND, :] = lo[...].astype(F32)
-    shifted[half : half + AHEAD, :] = up[...].astype(F32)
+    below = range(behind_windows)
+    above = range(inner[-1] + 1, count)
     first = BEHIND + half
     span = half + AHEAD
-    moved = shifted[pl.ds(cap - live, span), :]
-    row_ids = lax.broadcasted_iota(jnp.int32, (span, ca), 0) + first
-    ext[first : BEHIND + cap, :] = jnp.where(
-        row_ids[:half] < BEHIND + live, ext[first : BEHIND + cap, :], moved[:half]
-    )
-    ext[BEHIND + cap :, :] = moved[half:]
-    low_kv = mm(ext[:BEHIND, :].astype(BF16), waqkv[:, ca:])
-    keys_s[:BEHIND, :] = low_kv[:, :ca]
-    values_s[:BEHIND, :] = low_kv[:, ca:]
-    high_kv = mm(ext[first:, :].astype(BF16), waqkv[:, ca:])
-    keys_s[first:, :] = high_kv[:, :ca]
-    values_s[first:, :] = high_kv[:, ca:]
-    for k in range(0, len(outer), GROUP):
-        attend(outer[k : k + GROUP])
-
-    need(waout, wagg)
+    attend(inner)
+    if rounds > 1:
+        hear(0)
+        tell(1)
+
+    def with_low():
+        rim_low()
+        low_kv = mm(lo[...], waqkv[:, ca:])
+        keys_s[:BEHIND, :] = low_kv[:, :ca]
+        values_s[:BEHIND, :] = low_kv[:, ca:]
+        attend(below)
+
+    def with_high():
+        rim_high()
+        shifted[half : half + AHEAD, :] = up[...].astype(F32)
+        moved = shifted[pl.ds(cap - live, span), :]
+        row_ids = lax.broadcasted_iota(jnp.int32, (half, ca), 0) + first
+        merged = jnp.where(row_ids < BEHIND + live, hs[half:cap, :], moved[:half])
+        high_rows = jnp.concatenate([merged, moved[half:]], axis=0).astype(BF16)
+        high_kv = mm(high_rows, waqkv[:, ca:])
+        keys_s[first:, :] = high_kv[:, :ca]
+        values_s[first:, :] = high_kv[:, ca:]
+        for k in range(0, len(above), GROUP):
+            attend(above[k : k + GROUP])
+
+    pl.when(core == 0)(with_high)
+    if rounds > 2:
+        hear(1)
+        tell(2)
+    with_low()
+    pl.when(core == 1)(with_high)
+    finish_rim()
     atom_mid = mid[...] + mm(att_s[...], waout[...])
     mid[...] = atom_mid
     spread = jnp.maximum(mm(atom_mid.astype(BF16), wagg[...]), 0.0).astype(BF16)
@@ -266,7 +296,7 @@
     part_down[:, ct:] = count_wide[down].astype(BF16)
     part_up[:, :ct] = partial[ahead].astype(BF16)
     part_up[:, ct:] = count_wide[ahead].astype(BF16)
-    receive_part, finish_part = exchange(1, part_up, from_low, part_down, from_high)
+    part_low, part_high, finish_part = exchange(1, part_up, from_low, part_down, from_high)
 
     need(tsingle)
     own_sum = partial[rows : 2 * rows]
@@ -275,34 +305,38 @@
     token_mid = tsingle[middle, :].astype(F32) + own_sum[middle] / jnp.maximum(own_count[middle], 1.0)
     early_all[pl.ds(me, 1)] = normalize(token_mid).astype(BF16)[None]
 
-    def block(kind, src, peer, sent):
-        view = (early_all, late_all)[kind].at[src]
+    messages = (early_all, late_all)
+
+    def block(kind, src, peer, arrived, count=None):
+        view = messages[kind].at[src if count is None else pl.ds(0, count)]
         return pltpu.make_async_remote_copy(
             src_ref=view,
             dst_ref=view,
-            send_sem=sent,
-            recv_sem=ag_recv.at[src, kind],
+            send_sem=local_sem.at[kind],
+            recv_sem=arrived,
             device_id={"row": peer},
             device_id_type=pl.DeviceIdType.MESH,
         )
 
-    def relay(kind, src, over, act):
+    def crossing(kind, zz):
+        return cross_late.at[zz] if kind else cross_early.at[0]
+
+    def relay(kind, src, over):
         if over:
-            act(block(kind, src, across, across_send.at[src // 4, kind]))
-        act(block(kind, src, partner, ag_send.at[src // 2, kind]))
-
-    def own_sends(kind, act):
-        for there, peer, way in line:
-            pl.when(there)(lambda peer=peer, way=way: act(block(kind, me, peer, line_send.at[way, kind])))
-        relay(kind, me, True, act)
-
-    def start(c):
-        c.start()
-
-    def end(c):
-        c.wait_send()
-
-    own_sends(0, start)
+            block(kind, src, across, crossing(kind, src // 4)).start()
+        block(kind, src, partner, pair_recv.at[0, kind]).start()
+
+    def own_sends(kind):
+        for there, peer, diagonal in (line if kind == 0 else line[2:-2] + line[-2:] + line[:2]):
+            arrived = crossing(kind, z) if diagonal else line_recv.at[z, kind]
+            pl.when(there)(lambda peer=peer, arrived=arrived: block(kind, me, peer, arrived).start())
+        relay(kind, me, True)
+
+    for step in range(min(rounds - 1, 2), rounds):
+        hear(step)
+        if step + 1 < rounds:
+            tell(step + 1)
+    own_sends(0)
 
     need(pmask, tbias)
     pair = 2 * rows
@@ -317,8 +351,10 @@
             bias_half[0, h, :, here] = jnp.where(front, one, pltpu.roll(two, pair, 1))
             bias_half[1, h, :, here] = jnp.where(front, pltpu.roll(one, pair, 1), two)
     mid_t = mid[...].T
-    need(wtqkv, wgate)
-    receive_part()
+    need(wtqkv, wgate, wtout, wback, wpos)
+    joint = mm(wtout[...], wback[...]).astype(BF16)
+    part_low()
+    part_high()
     low = from_low[...].astype(F32)
     high = from_high[...].astype(F32)
 
@@ -346,38 +382,38 @@
         axis=1,
     )
     late_all[pl.ds(me, 1)] = late.astype(BF16)[None]
-    own_sends(1, start)
+    own_sends(1)
 
     direct = []
-    crossed = []
     for d in range(1, depth):
-        over = d < ends
-        direct.append((z >= d, index_of(z - d, y, core), over))
-        direct.append((z + d < depth, index_of(z + d, y, core), over))
-    crossed.append((None, across, False))
-    for d in range(1, depth):
-        crossed.append((z >= d, index_of(z - d, 1 - y, core), False))
-        crossed.append((z + d < depth, index_of(z + d, 1 - y, core), False))
-    steps = direct + crossed
-
-    def arrive(kind, src, over):
-        block(kind, src, partner, ag_send.at[0, kind]).wait_recv()
-        relay(kind, src, over, start)
-
-    def leave(kind, src, over):
-        relay(kind, src, over, end)
-
-    def each(kind, some, visit):
-        for there, src, over in some:
-            if there is None:
-                visit(kind, src, over)
-            else:
-                pl.when(there)(lambda src=src, over=over: visit(kind, src, over))
-
-    def last_hops(column):
+        direct.append((z >= d, z - d, d < ends))
+        direct.append((z + d < depth, z + d, d < ends))
+
+    def arrive(kind, some):
+        for there, zz, over in some:
+            src = index_of(zz, y, core)
+
+            @pl.when(there)
+            def _(src=src, zz=zz, over=over):
+                block(kind, src, partner, line_recv.at[zz, kind]).wait_recv()
+                relay(kind, src, over)
+
+    def crossed_late(there, zz):
+        src = index_of(zz, 1 - y, core)
+
+        @pl.when(there)
+        def _():
+            block(1, src, partner, cross_late.at[zz]).wait_recv()
+            block(1, src, partner, pair_recv.at[1, 1]).start()
+
+    def crossed_early():
+        block(0, 0, across, cross_early.at[0], depth).wait_recv()
         for zz in range(depth):
-            for kind in range(2):
-                block(kind, index_of(zz, column, 1 - core), partner, ag_send.at[0, kind]).wait_recv()
+            block(0, index_of(zz, 1 - y, core), partner, pair_recv.at[1, 0]).start()
+
+    def last_hops(side):
+        for kind in range(2):
+            block(kind, 0, partner, pair_recv.at[side, kind], depth).wait_recv()
 
     first_row = lax.broadcasted_iota(jnp.int32, (margin, ct), 0) == 0
 
@@ -396,7 +432,7 @@
                 u_half[side, at + margin : at + 2 * margin, :] = jnp.where(first_row, row, tile).astype(BF16)
                 u_half[side, at + 2 * margin : at + rows - margin, :] = early_rows[margin:]
 
-    each(0, direct[:2], arrive)
+    arrive(0, direct[:2])
     tw = ct // TH
     tquery = (mm(u, wtqkv[:, :ct]) * (1.0 / tw**0.5)).astype(BF16)
     batches = []
@@ -410,41 +446,51 @@
         through = mm_t(wide, wtqkv[:, ct + left : ct + right]).astype(BF16)
         batches.append((first_head, left, right, lanes, through))
     gate = jax.nn.sigmoid(mm(u, wgate[...]))
-    each(0, direct[2:], arrive)
-    each(1, direct, arrive)
-    last_hops(y)
+    back_in = mm(token_in.astype(BF16), wback[...])
+    arrive(0, direct[2:])
+    arrive(1, direct)
+    crossed_early()
+    crossed_late(True, z)
+    last_hops(0)
     assemble(0, y)
 
-    def scored(side, column):
-        features = u_half[side]
+    def scored(features, column, some):
         bias = bias_half[column]
         scores = []
-        for first_head, _, _, _, through in batches:
+        for first_head, _, _, _, through in some:
             score = mm_t(through, features)
             scores.append(score + bias[first_head : first_head + BATCH].reshape(score.shape))
-        return features, scores
-
-    def valued(features, exps):
-        mixed = [mm(e.astype(BF16), features).astype(BF16) for e in exps]
-        return [
-            mm(m, wtqkv[:, 2 * ct + left : 2 * ct + right]) for m, (_, left, right, _, _) in zip(mixed, batches)
-        ]
-
-    features, scores = scored(0, y)
-    own_max = [jnp.max(score, axis=-1, keepdims=True) for score in scores]
-    exps = [jnp.exp(score - m) for score, m in zip(scores, own_max)]
-    own_total = [jnp.sum(e, axis=-1, keepdims=True) for e in exps]
-    for k, out in enumerate(valued(features, exps)):
-        own_out[k] = out
-    each(0, crossed, arrive)
-    each(1, crossed, arrive)
-    last_hops(1 - y)
+        return scores
+
+    def valued(e, features, left, right):
+        mixed = mm(e.astype(BF16), features).astype(BF16)
+        return mm(mixed, wtqkv[:, 2 * ct + left : 2 * ct + right])
+
+    features = u_half[0]
+    own_max = []
+    own_total = []
+    own_out = []
+    parts = len(batches) // 2
+    for k in range(0, len(batches), parts):
+        some = batches[k : k + parts]
+        scores = scored(features, y, some)
+        for (_, left, right, _, _), score in zip(some, scores):
+            largest = jnp.max(score, axis=-1, keepdims=True)
+            e = jnp.exp(score - largest)
+            own_max.append(largest)
+            own_total.append(jnp.sum(e, axis=-1, keepdims=True))
+            own_out.append(valued(e, features, left, right))
+        for d in range(1, depth):
+            if (k == 0) == (d == 1):
+                crossed_late(z >= d, z - d)
+                crossed_late(z + d < depth, z + d)
+    last_hops(1)
     assemble(1, 1 - y)
-    need(wtout, wback, wpos)
-    features, scores = scored(1, 1 - y)
+    features = u_half[1]
+    scores = scored(features, 1 - y, batches)
     all_max = [jnp.maximum(m, jnp.max(score, axis=-1, keepdims=True)) for score, m in zip(scores, own_max)]
     exps = [jnp.exp(score - m) for score, m in zip(scores, all_max)]
-    outs = valued(features, exps)
+    outs = [valued(e, features, left, right) for e, (_, left, right, _, _) in zip(exps, batches)]
     blocks = [None] * chunks
     for k, (_, left, right, lanes, _) in enumerate(batches):
         scale = jnp.exp(own_max[k] - all_max[k])
@@ -457,20 +503,18 @@
             part = total[:, 128 * c - left : 128 * (c + 1) - left]
             blocks[c] = part if blocks[c] is None else blocks[c] + part
     gated = (gate * jnp.concatenate(blocks, axis=1)).astype(BF16)
-    token_out = (token_in + mm(gated, wtout[...])).astype(BF16)
-    tout_ref[...] = token_out
-    near[rows : 2 * rows, :] = mm(token_out, wback[...]).astype(BF16)
+    near[rows : 2 * rows, :] = (back_in + mm(gated, joint)).astype(BF16)
     upper = near.at[2 * rows - margin : 2 * rows]
     lower = near.at[rows : rows + rim_rows]
-    receive_back, finish_back = exchange(
+    finish_part()
+    back_low, back_high, finish_back = exchange(
         2, upper, near.at[rows - margin : rows], lower, near.at[2 * rows : 2 * rows + rim_rows]
     )
-    finish_rim()
-    finish_part()
+    tout_ref[...] = (token_in + mm(gated, wtout[...])).astype(BF16)
     for kind in range(2):
-        own_sends(kind, end)
-        each(kind, steps, leave)
-    receive_back()
+        block(kind, 0, partner, pair_recv.at[0, kind], n - 1).wait_send()
+    back_low()
+    back_high()
     back_t = lax.dot_general(near[...], hot_s[...], (((0,), (0,)), ((), ())), preferred_element_type=F32)
     atom_last = mid_t + back_t
     center = atom_last - jnp.mean(atom_last, axis=0, keepdims=True)
@@ -522,7 +566,7 @@
             pltpu.VMEM((BEHIND, ca), BF16),
             pltpu.VMEM((AHEAD, ca), BF16),
             pltpu.VMEM((cap + AHEAD, ca), F32),
-            pltpu.VMEM((BEHIND + cap + AHEAD, ca), F32),
+            pltpu.VMEM((cap, ca), BF16),
             pltpu.VMEM((BEHIND + cap + AHEAD, ca), F32),
             pltpu.VMEM((BEHIND + cap + AHEAD, ca), F32),
             pltpu.VMEM((cap, ca), F32),
@@ -535,16 +579,15 @@
             pltpu.VMEM((n, 2 * margin, ct + 128), BF16),
             pltpu.VMEM((2, n * rows // 2, ct), BF16),
             pltpu.VMEM((2, TH, rows, n * rows // 2), F32),
-            pltpu.VMEM((TH // BATCH, BATCH * rows, 256), F32),
             pltpu.VMEM((3 * rows, cap), BF16),
             pltpu.VMEM((3 * rows, ca), BF16),
             pltpu.SemaphoreType.DMA((1 + len(big),)),
-            pltpu.SemaphoreType.DMA((6,)),
-            pltpu.SemaphoreType.DMA((6,)),
+            pltpu.SemaphoreType.DMA((4,)),
             pltpu.SemaphoreType.DMA((n // 4, 2)),
-            pltpu.SemaphoreType.DMA((n // 4, 2)),
-            pltpu.SemaphoreType.DMA((n // 2, 2)),
-            pltpu.SemaphoreType.DMA((n, 2)),
+            pltpu.SemaphoreType.DMA((1,)),
+            pltpu.SemaphoreType.DMA((n // 4,)),
+            pltpu.SemaphoreType.DMA((2, 2)),
+            pltpu.SemaphoreType.REGULAR((max(n // 4 - 1, 1),)),
         ],
         compiler_params=pltpu.CompilerParams(collective_id=0, has_side_effects=True, vmem_limit_bytes=VMEM_LIMIT),
     )(atom_counts, *(pltpu.with_memory_space_constraint(a, pltpu.HBM) for a in (window_offsets,) + big))

time: 27.5 us -> 26.3 us (0.956)
  Pallas kernels: 26 us -> 24.8 us
    pallas_call x1, Pallas kernels: 25.4 us -> 24.1 us  [on_device(): pl.pallas_call(lambda *refs: kernel(n, *refs), out_shape=tuple((pltpu.VME...]
where the time goes in v5:
time: 26.3 us; the launch traced here: 26.1 us
  Pallas kernels  24.8 us (94%)
  between operations  1.29 us (5%)
    pallas_call x1, Pallas kernels, on_device(): pl.pallas_call(lambda *refs: kernel(n, *refs), out_shape=tuple((pltpu.VME...  24.1 us
    pallas_call x1, Pallas kernels, on_device(): pl.pallas_call(store, out_shape=tuple((jax.ShapeDtypeStruct(shape, kind)...  0.64 us

profile of v5, /device:TPU:1, one launch (start us, length us, event | category | flops | bytes accessed | tf_op | source)
XLA Modules:
  0.0 26.1 jit_solution(1231013773197228562)
XLA Ops:
  1.3 24.1 %shard_map.194 = (f32[3,384]{1,0:T(4,128)S(1)}, bf16[32,768]{1,0:T(8,128)(2,1)S(1)}) custom-call(s32[1]{0:T(128)S(6)} %copy.21.refs_0_, s32[12]{0:T(128)} %refs_1_.1, f32[3,384]{1,0:T(4,128)} %refs_2_.1, f32[3,384]{1,0:T(4,128)} %refs_3_.1, bf16[384,128]{1,0:T(8,128)(2,1)} %refs_4_.1, s32[384]{0:T(512)} %refs_5_.1, f32[4,384,128]{2,1,0:T(8,128)} %refs_6_.1, ...), custom_call_target="tpu_custom_call" | custom-call | tf_op jit(solution)/shard_map/pallas_call | solution.py:554
  25.4 0.6 %shard_map.195 = (f32[3,384]{1,0:T(4,128)}, bf16[32,768]{1,0:T(8,128)(2,1)}) custom-call(f32[3,384]{1,0:T(4,128)S(1)} %get-tuple-element.4.den, bf16[32,768]{1,0:T(8,128)(2,1)S(1)} %get-tuple-element.5.tout), custom_call_target="tpu_custom_call" | custom-call | tf_op jit(solution)/shard_map/pallas_call | solution.py:595

commit v6 on v5

--- a/solution.py
+++ b/solution.py
@@ -327,7 +327,7 @@
         block(kind, src, partner, pair_recv.at[0, kind]).start()
 
     def own_sends(kind):
-        for there, peer, diagonal in (line if kind == 0 else line[2:-2] + line[-2:] + line[:2]):
+        for there, peer, diagonal in (line[:-2] if kind == 0 else line[2:-2] + line[-2:] + line[:2]):
             arrived = crossing(kind, z) if diagonal else line_recv.at[z, kind]
             pl.when(there)(lambda peer=peer, arrived=arrived: block(kind, me, peer, arrived).start())
         relay(kind, me, True)
@@ -396,7 +396,7 @@
             @pl.when(there)
             def _(src=src, zz=zz, over=over):
                 block(kind, src, partner, line_recv.at[zz, kind]).wait_recv()
-                relay(kind, src, over)
+                relay(kind, src, over or kind == 0)
 
     def crossed_late(there, zz):
         src = index_of(zz, 1 - y, core)
@@ -449,7 +449,6 @@
     back_in = mm(token_in.astype(BF16), wback[...])
     arrive(0, direct[2:])
     arrive(1, direct)
-    crossed_early()
     crossed_late(True, z)
     last_hops(0)
     assemble(0, y)
@@ -470,20 +469,17 @@
     own_max = []
     own_total = []
     own_out = []
-    parts = len(batches) // 2
-    for k in range(0, len(batches), parts):
-        some = batches[k : k + parts]
-        scores = scored(features, y, some)
-        for (_, left, right, _, _), score in zip(some, scores):
-            largest = jnp.max(score, axis=-1, keepdims=True)
-            e = jnp.exp(score - largest)
-            own_max.append(largest)
-            own_total.append(jnp.sum(e, axis=-1, keepdims=True))
-            own_out.append(valued(e, features, left, right))
-        for d in range(1, depth):
-            if (k == 0) == (d == 1):
-                crossed_late(z >= d, z - d)
-                crossed_late(z + d < depth, z + d)
+    scores = scored(features, y, batches)
+    for score in scores:
+        own_max.append(jnp.max(score, axis=-1, keepdims=True))
+    exps = [jnp.exp(score - m) for score, m in zip(scores, own_max)]
+    for (_, left, right, _, _), e in zip(batches, exps):
+        own_total.append(jnp.sum(e, axis=-1, keepdims=True))
+        own_out.append(valued(e, features, left, right))
+    crossed_early()
+    for d in range(1, depth):
+        crossed_late(z >= d, z - d)
+        crossed_late(z + d < depth, z + d)
     last_hops(1)
     assemble(1, 1 - y)
     features = u_half[1]

time: 26.3 us -> 25.9 us (0.985)
  Pallas kernels: 24.8 us -> 24.4 us
    pallas_call x1, Pallas kernels: 24.1 us -> 23.7 us  [on_device(): pl.pallas_call(lambda *refs: kernel(n, *refs), out_shape=tuple((pltpu.VME...]
where the time goes in v6:
time: 25.9 us; the launch traced here: 25.6 us
  Pallas kernels  24.4 us (94%)
  between operations  1.29 us (5%)
    pallas_call x1, Pallas kernels, on_device(): pl.pallas_call(lambda *refs: kernel(n, *refs), out_shape=tuple((pltpu.VME...  23.7 us
    pallas_call x1, Pallas kernels, on_device(): pl.pallas_call(store, out_shape=tuple((jax.ShapeDtypeStruct(shape, kind)...  0.64 us

profile of v6, /device:TPU:1, one launch (start us, length us, event | category | flops | bytes accessed | tf_op | source)
XLA Modules:
  0.0 25.6 jit_solution(9479394904145793672)
XLA Ops:
  1.3 23.7 %shard_map.194 = (f32[3,384]{1,0:T(4,128)S(1)}, bf16[32,768]{1,0:T(8,128)(2,1)S(1)}) custom-call(s32[1]{0:T(128)S(6)} %copy.21.refs_0_, s32[12]{0:T(128)} %refs_1_.1, f32[3,384]{1,0:T(4,128)} %refs_2_.1, f32[3,384]{1,0:T(4,128)} %refs_3_.1, bf16[384,128]{1,0:T(8,128)(2,1)} %refs_4_.1, s32[384]{0:T(512)} %refs_5_.1, f32[4,384,128]{2,1,0:T(8,128)} %refs_6_.1, ...), custom_call_target="tpu_custom_call" | custom-call | tf_op jit(solution)/shard_map/pallas_call | solution.py:550
  25.0 0.6 %shard_map.195 = (f32[3,384]{1,0:T(4,128)}, bf16[32,768]{1,0:T(8,128)(2,1)}) custom-call(f32[3,384]{1,0:T(4,128)S(1)} %get-tuple-element.4.den, bf16[32,768]{1,0:T(8,128)(2,1)S(1)} %get-tuple-element.5.tout), custom_call_target="tpu_custom_call" | custom-call | tf_op jit(solution)/shard_map/pallas_call | solution.py:591

commit v7 on v6

--- a/solution.py
+++ b/solution.py
@@ -20,7 +20,7 @@
 
 F32 = jnp.float32
 BF16 = jnp.bfloat16
-GROUP = 4
+GROUP = 8
 BATCH = 4
 VMEM_LIMIT = 40 * 1024 * 1024
 
@@ -93,13 +93,9 @@
     across = index_of(z, 1 - y, core)
     line = []
     for d in range(1, depth):
-        line.append((z + d < depth, index_of(z + d, y, core), False))
-        line.append((z >= d, index_of(z - d, y, core), False))
-
-    ends = depth - 1
-    if ends:
-        line.append((z == 0, index_of(z + ends, 1 - y, core), True))
-        line.append((z == ends, index_of(z - ends, 1 - y, core), True))
+        line.append((z + d < depth, index_of(z + d, y, core)))
+        line.append((z >= d, index_of(z - d, y, core)))
+
 
     barrier = pltpu.get_barrier_semaphore()
 
@@ -194,7 +190,7 @@
     def hear(step):
         pl.semaphore_wait(ready.at[step], links)
 
-    rounds = depth - 1
+    rounds = max(depth - 2, 0)
     if rounds:
         tell(0)
     need(waqkv)
@@ -318,21 +314,16 @@
             device_id_type=pl.DeviceIdType.MESH,
         )
 
-    def crossing(kind, zz):
-        return cross_late.at[zz] if kind else cross_early.at[0]
-
-    def relay(kind, src, over):
-        if over:
-            block(kind, src, across, crossing(kind, src // 4)).start()
+    def relay(kind, src):
+        block(kind, src, across, cross_late.at[src // 4] if kind else cross_early.at[0]).start()
         block(kind, src, partner, pair_recv.at[0, kind]).start()
 
     def own_sends(kind):
-        for there, peer, diagonal in (line[:-2] if kind == 0 else line[2:-2] + line[-2:] + line[:2]):
-            arrived = crossing(kind, z) if diagonal else line_recv.at[z, kind]
-            pl.when(there)(lambda peer=peer, arrived=arrived: block(kind, me, peer, arrived).start())
-        relay(kind, me, True)
-
-    for step in range(min(rounds - 1, 2), rounds):
+        for there, peer in line[::-1] if kind else line:
+            pl.when(there)(lambda peer=peer: block(kind, me, peer, line_recv.at[z, kind]).start())
+        relay(kind, me)
+
+    for step in range(max(min(rounds - 1, 2), 0), rounds):
         hear(step)
         if step + 1 < rounds:
             tell(step + 1)
@@ -386,17 +377,17 @@
 
     direct = []
     for d in range(1, depth):
-        direct.append((z >= d, z - d, d < ends))
-        direct.append((z + d < depth, z + d, d < ends))
+        direct.append((z >= d, z - d))
+        direct.append((z + d < depth, z + d))
 
     def arrive(kind, some):
-        for there, zz, over in some:
+        for there, zz in some:
             src = index_of(zz, y, core)
 
             @pl.when(there)
-            def _(src=src, zz=zz, over=over):
+            def _(src=src, zz=zz):
                 block(kind, src, partner, line_recv.at[zz, kind]).wait_recv()
-                relay(kind, src, over or kind == 0)
+                relay(kind, src)
 
     def crossed_late(there, zz):
         src = index_of(zz, 1 - y, core)
@@ -583,7 +574,7 @@
             pltpu.SemaphoreType.DMA((1,)),
             pltpu.SemaphoreType.DMA((n // 4,)),
             pltpu.SemaphoreType.DMA((2, 2)),
-            pltpu.SemaphoreType.REGULAR((max(n // 4 - 1, 1),)),
+            pltpu.SemaphoreType.REGULAR((max(n // 4 - 2, 1),)),
         ],
         compiler_params=pltpu.CompilerParams(collective_id=0, has_side_effects=True, vmem_limit_bytes=VMEM_LIMIT),
     )(atom_counts, *(pltpu.with_memory_space_constraint(a, pltpu.HBM) for a in (window_offsets,) + big))

time: 25.9 us -> 25.2 us (0.973)
  Pallas kernels: 24.4 us -> 23.7 us
    pallas_call x1, Pallas kernels: 23.7 us -> 23.1 us  [on_device(): pl.pallas_call(lambda *refs: kernel(n, *refs), out_shape=tuple((pltpu.VME...]
where the time goes in v7:
time: 25.2 us; the launch traced here: 25 us
  Pallas kernels  23.7 us (94%)
  between operations  1.29 us (5%)
    pallas_call x1, Pallas kernels, on_device(): pl.pallas_call(lambda *refs: kernel(n, *refs), out_shape=tuple((pltpu.VME...  23.1 us
    pallas_call x1, Pallas kernels, on_device(): pl.pallas_call(store, out_shape=tuple((jax.ShapeDtypeStruct(shape, kind)...  0.64 us

profile of v7, /device:TPU:1, one launch (start us, length us, event | category | flops | bytes accessed | tf_op | source)
XLA Modules:
  0.0 25.0 jit_solution(9564864096040053726)
XLA Ops:
  1.3 23.1 %shard_map.194 = (f32[3,384]{1,0:T(4,128)S(1)}, bf16[32,768]{1,0:T(8,128)(2,1)S(1)}) custom-call(s32[1]{0:T(128)S(6)} %copy.21.refs_0_, s32[12]{0:T(128)} %refs_1_.1, f32[3,384]{1,0:T(4,128)} %refs_2_.1, f32[3,384]{1,0:T(4,128)} %refs_3_.1, bf16[384,128]{1,0:T(8,128)(2,1)} %refs_4_.1, s32[384]{0:T(512)} %refs_5_.1, f32[4,384,128]{2,1,0:T(8,128)} %refs_6_.1, ...), custom_call_target="tpu_custom_call" | custom-call | tf_op jit(solution)/shard_map/pallas_call | solution.py:541
  24.4 0.6 %shard_map.195 = (f32[3,384]{1,0:T(4,128)}, bf16[32,768]{1,0:T(8,128)(2,1)}) custom-call(f32[3,384]{1,0:T(4,128)S(1)} %get-tuple-element.4.den, bf16[32,768]{1,0:T(8,128)(2,1)S(1)} %get-tuple-element.5.tout), custom_call_target="tpu_custom_call" | custom-call | tf_op jit(solution)/shard_map/pallas_call | solution.py:582

commit v8 on v7

--- a/solution.py
+++ b/solution.py
@@ -241,6 +241,19 @@
     above = range(inner[-1] + 1, count)
     first = BEHIND + half
     span = half + AHEAD
+    slot_lane = lax.broadcasted_iota(jnp.int32, (1, cap), 1)
+    living = slot_lane < live
+    sub_ids = lax.broadcasted_iota(jnp.int32, (3 * rows, cap), 0)
+    hot = ((sub_ids == relative) & living).astype(F32)
+    counted = jnp.sum(hot, axis=-1, keepdims=True)
+    hot_s[...] = hot.astype(BF16)
+    few = jnp.minimum(counted, 256.0)
+    lane_c = lax.broadcasted_iota(jnp.int32, (3 * rows, 128), 1)
+    count_wide = jnp.where(lane_c < 64, few, counted - few)
+    down = slice(rows - margin, rows)
+    ahead = slice(2 * rows, 2 * rows + rim_rows)
+    part_down[:, ct:] = count_wide[down].astype(BF16)
+    part_up[:, ct:] = count_wide[ahead].astype(BF16)
     attend(inner)
     if rounds > 1:
         hear(0)
@@ -276,22 +289,9 @@
     atom_mid = mid[...] + mm(att_s[...], waout[...])
     mid[...] = atom_mid
     spread = jnp.maximum(mm(atom_mid.astype(BF16), wagg[...]), 0.0).astype(BF16)
-    slot_lane = lax.broadcasted_iota(jnp.int32, (1, cap), 1)
-    living = slot_lane < live
-    sub_ids = lax.broadcasted_iota(jnp.int32, (3 * rows, cap), 0)
-    hot = ((sub_ids == relative) & living).astype(F32)
-    counted = jnp.sum(hot, axis=-1, keepdims=True)
-    hot_s[...] = hot.astype(BF16)
     partial = mm(hot_s[...], spread)
-    few = jnp.minimum(counted, 256.0)
-    lane_c = lax.broadcasted_iota(jnp.int32, (3 * rows, 128), 1)
-    count_wide = jnp.where(lane_c < 64, few, counted - few)
-    down = slice(rows - margin, rows)
-    ahead = slice(2 * rows, 2 * rows + rim_rows)
     part_down[:, :ct] = partial[down].astype(BF16)
-    part_down[:, ct:] = count_wide[down].astype(BF16)
     part_up[:, :ct] = partial[ahead].astype(BF16)
-    part_up[:, ct:] = count_wide[ahead].astype(BF16)
     part_low, part_high, finish_part = exchange(1, part_up, from_low, part_down, from_high)
 
     need(tsingle)
@@ -467,10 +467,10 @@
     for (_, left, right, _, _), e in zip(batches, exps):
         own_total.append(jnp.sum(e, axis=-1, keepdims=True))
         own_out.append(valued(e, features, left, right))
-    crossed_early()
     for d in range(1, depth):
         crossed_late(z >= d, z - d)
         crossed_late(z + d < depth, z + d)
+    crossed_early()
     last_hops(1)
     assemble(1, 1 - y)
     features = u_half[1]

time: 25.2 us -> 25.2 us (level)
  no operation moved by 1% of the time
where the time goes in v8:
time: 25.2 us; the launch traced here: 25 us
  Pallas kernels  23.7 us (94%)
  between operations  1.29 us (5%)
    pallas_call x1, Pallas kernels, on_device(): pl.pallas_call(lambda *refs: kernel(n, *refs), out_shape=tuple((pltpu.VME...  23.1 us
    pallas_call x1, Pallas kernels, on_device(): pl.pallas_call(store, out_shape=tuple((jax.ShapeDtypeStruct(shape, kind)...  0.64 us

profile of v8, /device:TPU:1, one launch (start us, length us, event | category | flops | bytes accessed | tf_op | source)
XLA Modules:
  0.0 25.0 jit_solution(2070712639218293427)
XLA Ops:
  1.3 23.1 %shard_map.194 = (f32[3,384]{1,0:T(4,128)S(1)}, bf16[32,768]{1,0:T(8,128)(2,1)S(1)}) custom-call(s32[1]{0:T(128)S(6)} %copy.21.refs_0_, s32[12]{0:T(128)} %refs_1_.1, f32[3,384]{1,0:T(4,128)} %refs_2_.1, f32[3,384]{1,0:T(4,128)} %refs_3_.1, bf16[384,128]{1,0:T(8,128)(2,1)} %refs_4_.1, s32[384]{0:T(512)} %refs_5_.1, f32[4,384,128]{2,1,0:T(8,128)} %refs_6_.1, ...), custom_call_target="tpu_custom_call" | custom-call | tf_op jit(solution)/shard_map/pallas_call | solution.py:541
  24.4 0.6 %shard_map.195 = (f32[3,384]{1,0:T(4,128)}, bf16[32,768]{1,0:T(8,128)(2,1)}) custom-call(f32[3,384]{1,0:T(4,128)S(1)} %get-tuple-element.4.den, bf16[32,768]{1,0:T(8,128)(2,1)S(1)} %get-tuple-element.5.tout), custom_call_target="tpu_custom_call" | custom-call | tf_op jit(solution)/shard_map/pallas_call | solution.py:582

commit v9 on v8

--- a/solution.py
+++ b/solution.py
@@ -52,7 +52,7 @@
     den_ref, tout_ref,
     offsets_s,
     pos, noise, single, token, abias, tsingle, tbias, pmask,
-    wcoord, waqkv, waout, wagg, wtqkv, wgate, wtout, wback, wpos,
+    wcoord, atom_w, token_w, wpos,
     columns, hs, tail, head, lo, up, shifted, queries, keys_s, values_s, mid, att_s,
     part_down, part_up, from_low, from_high, early_all, late_all, u_half, bias_half, hot_s, near,
     local_sem, edge_recv, line_recv, cross_early, cross_late, pair_recv, ready,
@@ -66,16 +66,27 @@
     has_low = me > 0
     has_high = me < last
 
+    ends_at = (3 * ca, 4 * ca, 4 * ca + ct)
+    waqkv, waout, wagg = (atom_w.at[:, a:b] for a, b in zip((0,) + ends_at, ends_at))
+    ends_at = (3 * ct, 4 * ct, 5 * ct, 5 * ct + ca)
+    wtqkv, wgate, wtout, wback = (token_w.at[:, a:b] for a, b in zip((0,) + ends_at, ends_at))
+    joined = [
+        (atom_w, [(waqkv_h, waqkv), (waout_h, waout), (wagg_h, wagg)]),
+        (token_w, [(wtqkv_h, wtqkv), (wgate_h, wgate), (wtout_h, wtout), (wback_h, wback)]),
+    ]
     pairs = [
         (pos_h, pos), (noise_h, noise), (single_h, single), (wcoord_h, wcoord), (token_h, token),
-        (waqkv_h, waqkv), (abias_h, abias), (waout_h, waout), (wagg_h, wagg), (tsingle_h, tsingle),
-        (wtqkv_h, wtqkv), (wgate_h, wgate), (mask_h, pmask), (tbias_h, tbias), (wtout_h, wtout),
-        (wback_h, wback), (wpos_h, wpos), (offsets_h, offsets_s),
+        (abias_h, abias), (tsingle_h, tsingle),
+        (mask_h, pmask), (tbias_h, tbias),
+        (wpos_h, wpos), (offsets_h, offsets_s),
     ]
     copies = {}
-    for k, (src, dst) in enumerate(pairs):
-        copies[id(dst)] = pltpu.make_async_copy(src, dst, local_sem.at[k])
-        copies[id(dst)].start()
+    order = [(k, dst, [(src, dst)]) for k, (src, dst) in enumerate(pairs)]
+    group = [(len(pairs) + k, whole, parts) for k, (whole, parts) in enumerate(joined)]
+    for k, whole, parts in order[:5] + group[:1] + order[5:7] + group[1:] + order[7:]:
+        for src, dst in parts:
+            pltpu.make_async_copy(src, dst, local_sem.at[k]).start()
+        copies[id(whole)] = pltpu.make_async_copy(whole, whole, local_sem.at[k])
 
     def need(*refs):
         for r in refs:
@@ -193,7 +204,7 @@
     rounds = max(depth - 2, 0)
     if rounds:
         tell(0)
-    need(waqkv)
+    need(atom_w)
     hw = ca // AH
     normed_b = normed.astype(BF16)
     own = mm(normed_b, waqkv[...])
@@ -201,7 +212,7 @@
     head_lanes = [lanes_between(ca, h * hw, (h + 1) * hw) for h in range(AH)]
     keys_s[BEHIND : BEHIND + cap, :] = own[:, ca : 2 * ca]
     values_s[BEHIND : BEHIND + cap, :] = own[:, 2 * ca :]
-    need(abias, offsets_s, waout, wagg)
+    need(abias, offsets_s)
 
     top = jnp.where(has_high, BEHIND + live + AHEAD, BEHIND + live)
     bottom = jnp.where(has_low, 0, BEHIND)
@@ -342,7 +353,7 @@
             bias_half[0, h, :, here] = jnp.where(front, one, pltpu.roll(two, pair, 1))
             bias_half[1, h, :, here] = jnp.where(front, pltpu.roll(one, pair, 1), two)
     mid_t = mid[...].T
-    need(wtqkv, wgate, wtout, wback, wpos)
+    need(token_w, wpos)
     joint = mm(wtout[...], wback[...]).astype(BF16)
     part_low()
     part_high()
@@ -544,7 +555,9 @@
         in_specs=[pl.BlockSpec(memory_space=pltpu.SMEM)] + [hbm] * (1 + len(big)),
         out_specs=(vmem, vmem),
         scratch_shapes=[pltpu.SMEM(window_offsets.shape, jnp.int32)]
-        + [pltpu.VMEM(a.shape, a.dtype) for a in big]
+        + [pltpu.VMEM(a.shape, a.dtype) for a in big[:9]]
+        + [pltpu.VMEM((ca, 4 * ca + ct), BF16), pltpu.VMEM((ct, 5 * ct + ca), BF16)]
+        + [pltpu.VMEM(w_pos.shape, w_pos.dtype)]
         + [
             pltpu.VMEM((128, cap), F32),
             pltpu.VMEM((cap, ca), F32),
@@ -568,7 +581,7 @@
             pltpu.VMEM((2, TH, rows, n * rows // 2), F32),
             pltpu.VMEM((3 * rows, cap), BF16),
             pltpu.VMEM((3 * rows, ca), BF16),
-            pltpu.SemaphoreType.DMA((1 + len(big),)),
+            pltpu.SemaphoreType.DMA((len(big) - 4,)),
             pltpu.SemaphoreType.DMA((4,)),
             pltpu.SemaphoreType.DMA((n // 4, 2)),
             pltpu.SemaphoreType.DMA((1,)),

time: 25.2 us -> 25.2 us (level)
  no operation moved by 1% of the time
where the time goes in v9:
time: 25.2 us; the launch traced here: 25 us
  Pallas kernels  23.7 us (94%)
  between operations  1.29 us (5%)
    pallas_call x1, Pallas kernels, on_device(): pl.pallas_call(lambda *refs: kernel(n, *refs), out_shape=tuple((pltpu.VME...  23 us
    pallas_call x1, Pallas kernels, on_device(): pl.pallas_call(store, out_shape=tuple((jax.ShapeDtypeStruct(shape, kind)...  0.64 us

profile of v9, /device:TPU:1, one launch (start us, length us, event | category | flops | bytes accessed | tf_op | source)
XLA Modules:
  0.0 25.0 jit_solution(4060912376923091679)
XLA Ops:
  1.3 23.0 %shard_map.194 = (f32[3,384]{1,0:T(4,128)S(1)}, bf16[32,768]{1,0:T(8,128)(2,1)S(1)}) custom-call(s32[1]{0:T(128)S(6)} %copy.21.refs_0_, s32[12]{0:T(128)} %refs_1_.1, f32[3,384]{1,0:T(4,128)} %refs_2_.1, f32[3,384]{1,0:T(4,128)} %refs_3_.1, bf16[384,128]{1,0:T(8,128)(2,1)} %refs_4_.1, s32[384]{0:T(512)} %refs_5_.1, f32[4,384,128]{2,1,0:T(8,128)} %refs_6_.1, ...), custom_call_target="tpu_custom_call" | custom-call | tf_op jit(solution)/shard_map/pallas_call | solution.py:552
  24.3 0.6 %shard_map.195 = (f32[3,384]{1,0:T(4,128)}, bf16[32,768]{1,0:T(8,128)(2,1)}) custom-call(f32[3,384]{1,0:T(4,128)S(1)} %get-tuple-element.4.den, bf16[32,768]{1,0:T(8,128)(2,1)S(1)} %get-tuple-element.5.tout), custom_call_target="tpu_custom_call" | custom-call | tf_op jit(solution)/shard_map/pallas_call | solution.py:595
